TPU v7x, 128 devices: a whole 4x4x4 slice. The times are simulated.
128 devices in a mesh: lon: 16 (over y, z_hi, core), lat: 8 (over z_lo, x).
Axes of the slice: x: 4, y: 4, z: 4 (z_hi: 2, z_lo: 2; z = z_hi * 2 + z_lo), core: 2. Of those that a mesh axis runs over, the one named last changes fastest.
Arguments:
- members: bfloat16 [3, 256, 2880, 128], P(None, 'lat', 'lon'), may hold values from -6 to 6
- background: bfloat16 [3, 256, 2880], P(None, 'lat', 'lon'), may hold values from -6 to 6
Outputs:
- modes: float32 [3, 256, 2880, 128], P(None, 'lat', 'lon')
- r_factor: float32 [128, 128], replicated
All inputs are finite; a program needn't handle non-finite values.
Results may differ from a plain program's by a relative error of at most 0.0076.
The roundings to bfloat16 on the way count: a program that leaves them out, or rounds other values in their place, can miss the bound.
Values may be sent and summed in bfloat16 or wider, within the bound.
A program may use at most 64 MiB of HBM per device.

v0:
```python
import math

import jax
import jax.numpy as jnp
from jax import lax
from jax.sharding import PartitionSpec as P


def extended(shard, sides, width, wrap):
    for axis, dim in sides:
        peers, length = (lax.axis_size(axis), shard.shape[dim])
        up = [(i, (i + 1) % peers) for i in range(peers if wrap else peers - 1)]
        down = [(j, i) for i, j in up]
        last = lax.slice_in_dim(shard, length - width, length, axis=dim)
        leading = lax.slice_in_dim(shard, 0, width, axis=dim)
        before = lax.ppermute(last, axis, up)
        after = lax.ppermute(leading, axis, down)
        shard = jnp.concatenate([before, shard, after], axis=dim)
    return shard


def row_coefs(glob, nlat):
    phi = (0.125 * (glob.astype(jnp.float32) + 0.5) - 0.0625 * nlat) * (math.pi / 180.0)
    kx = 0.05 + 0.2 * (1.0 - jnp.cos(phi))
    weight = jnp.sqrt(jnp.cos(phi))
    return (kx, weight)


def smooth_pass(padded, kx):
    centre = padded[:, 1:-1, 1:-1]
    east_west = padded[:, 1:-1, 2:] + padded[:, 1:-1, :-2] - 2.0 * centre
    north_south = padded[:, 2:, 1:-1] + padded[:, :-2, 1:-1] - 2.0 * centre
    return centre + kx[None, :, None, None] * east_west + 0.2 * north_south


def chol_upper(gram):
    order = gram.shape[0]
    index = jnp.arange(order)

    def column(j, lower):
        row_j = lax.dynamic_slice_in_dim(lower, j, 1, 0)[0]
        col_g = lax.dynamic_slice_in_dim(gram, j, 1, 1)[:, 0]
        resid = col_g - jnp.dot(lower, row_j, precision=lax.Precision.HIGHEST)
        pivot = jnp.sqrt(jnp.sum(jnp.where(index == j, resid, 0.0)))
        col_new = jnp.where(index >= j, resid / pivot, 0.0)
        return lower + col_new[:, None] * (index[None, :] == j).astype(jnp.float32)

    lower = lax.fori_loop(0, order, column, jnp.zeros((order, order), jnp.float32))
    return lower.T


def upper_inverse(upper):
    order = upper.shape[0]
    index = jnp.arange(order)
    ident = jnp.eye(order, dtype=jnp.float32)

    def row_step(step, solved):
        i = order - 1 - step
        row_u = lax.dynamic_slice_in_dim(upper, i, 1, 0)[0]
        diag = jnp.sum(jnp.where(index == i, row_u, 0.0))
        above = jnp.where(index > i, row_u, 0.0)
        unit = lax.dynamic_slice_in_dim(ident, i, 1, 0)[0]
        new_row = (unit - jnp.dot(above, solved, precision=lax.Precision.HIGHEST)) / diag
        return solved + (index == i).astype(jnp.float32)[:, None] * new_row[None, :]

    return lax.fori_loop(0, order, row_step, jnp.zeros((order, order), jnp.float32))


def local(members, background):
    fields, rows, cols, width = members.shape
    nlat = rows * lax.axis_size("lat")
    first = lax.axis_index("lat") * rows
    kx_rows, unused_weight = row_coefs(first + jnp.arange(rows), nlat)
    padded = extended(members, (("lat", 1),), 1, False)
    padded = extended(padded, (("lon", 2),), 1, True)
    inner = smooth_pass(padded.astype(jnp.float32), kx_rows)
    padded = extended(inner, (("lat", 1),), 1, False)
    padded = extended(padded, (("lon", 2),), 1, True)
    final = smooth_pass(padded, kx_rows)
    unused_kx, weight = row_coefs(first + jnp.arange(rows), nlat)
    anomaly = (
        (final - background.astype(jnp.float32)[:, :, :, None]) * weight[None, :, None, None]
    ).astype(jnp.bfloat16)
    matrix = anomaly.reshape(-1, width)
    partial_gram = lax.dot_general(
        matrix, matrix, (((0,), (0,)), ((), ())), preferred_element_type=jnp.float32
    )
    gram = lax.psum(partial_gram, "lat")
    gram = lax.psum(gram, "lon")
    total_rows = fields * nlat * cols * lax.axis_size("lon")
    gram = gram / total_rows
    r_factor = chol_upper(gram)
    inverse = upper_inverse(r_factor)
    modes = jnp.dot(
        matrix, inverse, precision=lax.Precision.HIGHEST, preferred_element_type=jnp.float32
    )
    return (modes.reshape(fields, rows, cols, width), r_factor)


def solution(mesh):
    return jax.shard_map(
        local,
        mesh=mesh,
        in_specs=(P(None, "lat", "lon", None), P(None, "lat", "lon")),
        out_specs=(P(None, "lat", "lon", None), P()),
        check_vma=False,
    )
```

profile of v0, /device:TPU:1, one launch (start us, length us, event | category | flops | bytes accessed | tf_op | source)
XLA Modules:
  0.0 709.0 jit_solution(13157840494007377491)
XLA Ops:
  7.2 2.0 fusion.45
  9.3 4.0 collective-permute-start
  13.3 1.3 collective-permute-start.1
  14.6 1.0 collective-permute-done
  15.6 4.3 constant_dynamic-update-slice_fusion.1
  20.0 5.1 collective-permute-start.2
  25.2 1.2 collective-permute-done.2
  26.3 3.8 collective-permute-done.3
  30.2 2.0 maximum_convert_fusion
  32.1 5.8 fusion.34
  38.0 4.1 collective-permute-start.4
  42.1 1.3 collective-permute-start.5
  43.4 4.3 collective-permute-done.4
  47.8 4.1 collective-permute-done.5
  52.2 3.1 collective-permute-start.7
  55.4 1.7 collective-permute-done.6
  57.1 14.0 %fusion.27 = bf16[3,32,180,128]{3,2,1,0:T(8,128)(2,1)S(1)} fusion(f32[3,32,180,128]{3,2,1,0:T(8,128)S(1)} %fusion.34, f32[3,1,180,128]{3,2,1,0:T(8,128)S(1)} %collective-permute-done.4, f32[3,1,180,128]{3,2,1,0:T(8,128)S(1)} %collective-permute-done.5, f32[3,34,1,128]{3,2,1,0:T(1,128)S(1)} %collective-permute-done.7, ...), kind=kLoop, calls=%fused_computation.37 | loop fusion | flops 44236800 | bytes 13997824 | tf_op jit(solution)/shard_map/convert_element_type | solution.py:83
  71.2 2.1 copy-done
  73.2 2.0 convolution_bitcast_fusion.2
  75.5 74.0 %all-reduce.3.cloned.1.call-done = f32[128,128]{1,0:T(8,128)} async-done(((f32[128,128]{1,0:T(8,128)}), f32[128,128]{1,0:T(8,128)}) %all-reduce.3.cloned.1.call-update) | async-done | bytes 65552 | tf_op jit(solution)/shard_map/psum | solution.py:88
  149.5 132.7 %all-reduce.5.cloned.1.call-done = f32[128,128]{1,0:T(8,128)} async-done(((f32[128,128]{1,0:T(8,128)}), f32[128,128]{1,0:T(8,128)}) %all-reduce.5.cloned.1.call-update) | async-done | bytes 65552 | tf_op jit(solution)/shard_map/psum | solution.py:89
  283.2 213.3 %while.32 = (s32[]{:T(128)}, f32[128,128]{1,0:T(8,128)S(1)}, f32[128,128]{0,1:T(8,128)S(1)}, s32[]{:T(128)}, s32[]{:T(128)}) while((s32[]{:T(128)}, f32[128,128]{1,0:T(8,128)S(1)}, f32[128,128]{0,1:T(8,128)S(1)}, s32[]{:T(128)}, s32[]{:T(128)}) %tuple.88), condition=%wide.region_4.5_spmd.clone.clone, body=%wide.region_2.4_spmd.clone.clone.sunk | while | flops 263298 | bytes 333408 | solution.py:48
  496.6 197.9 %while.33 = (s32[]{:T(128)}, f32[128,128]{1,0:T(8,128)S(1)}, f32[128,128]{1,0:T(8,128)S(1)}, f32[128,128]{1,0:T(8,128)S(1)}, s32[]{:T(128)}, /*index=5*/s32[]{:T(128)}, s32[]{:T(128)}, s32[]{:T(128)}) while((s32[]{:T(128)}, f32[128,128]{1,0:T(8,128)S(1)}, f32[128,128]{1,0:T(8,128)S(1)}, f32[128,128]{1,0:T(8,128)S(1)}, ...), condition=%wide.region_7.8_spmd.clone.clone, body=%wide.region_5.7_spmd.clone.clone.sunk | while | flops 263302 | bytes 202401 | solution.py:66
  694.5 7.7 %fusion.38 = f32[3,32,180,128]{3,1,2,0:T(8,128)} fusion(bf16[3,32,180,128]{3,2,1,0:T(8,128)(2,1)} %copy-done, f32[128,128]{1,0:T(8,128)S(1)} %get-tuple-element.220), kind=kOutput, calls=%fused_computation.58 | convolution fusion | flops 3397386240 | bytes 13336576 | tf_op jit(solution)/shard_map/dot_general | solution.py:94
  (1181 shorter events, 313.7 us)
Async XLA Ops:
  7.2 142.3 %all-reduce.3.cloned.1.call-start = ((), (), s32[]{:S(2)}) async-start(), calls=%async_computation | async-start | bytes 131072 | tf_op jit(solution)/shard_map/psum | solution.py:88
  9.3 6.3 collective-permute-start
  13.3 6.6 collective-permute-start.1
  20.0 6.3 collective-permute-start.2
  25.1 5.1 collective-permute-start.3
  38.0 17.4 %copy-start.2 = (bf16[3,32,180]{2,1,0:T(8,128)(2,1)S(1)}, bf16[3,32,180]{2,1,0:T(8,128)(2,1)}, u32[]{:S(2)}) copy-start(bf16[3,32,180]{2,1,0:T(8,128)(2,1)} %param.7) | copy-start | bytes 103684
  38.0 9.8 %collective-permute-start.4 = (f32[3,1,180,128]{3,2,1,0:T(8,128)S(1)}, f32[3,1,180,128]{3,2,1,0:T(8,128)S(1)}, u32[]{:S(2)}, u32[]{:S(2)}) collective-permute-start(f32[3,1,180,128]{3,2,1,0:T(8,128)S(1)} %get-tuple-element.307), channel_id=1, source_target_pairs={{0,1},{1,2},{2,3},{3,4},{4,5},{5,6},{6,7},{8,9},{9,10},{10,11},{11... | collective-permute-start | bytes 829448 | tf_op jit(solution)/shard_map/ppermute | solution.py:16
  42.1 9.7 %collective-permute-start.5 = (f32[3,1,180,128]{3,2,1,0:T(8,128)S(1)}, f32[3,1,180,128]{3,2,1,0:T(8,128)S(1)}, u32[]{:S(2)}, u32[]{:S(2)}) collective-permute-start(f32[3,1,180,128]{3,2,1,0:T(8,128)S(1)} %get-tuple-element.306), channel_id=1, source_target_pairs={{1,0},{2,1},{3,2},{4,3},{5,4},{6,5},{7,6},{9,8},{10,9},{11,10},{12... | collective-permute-start | bytes 829448 | tf_op jit(solution)/shard_map/ppermute | solution.py:17
  52.0 5.1 collective-permute-start.6
  52.2 5.0 collective-permute-start.7
  71.2 2.1 copy-start
  75.3 207.0 %all-reduce.5.cloned.1.call-start = ((), (), s32[]{:S(2)}) async-start(), calls=%async_computation.1 | async-start | bytes 131072 | tf_op jit(solution)/shard_map/psum | solution.py:89
  694.4 7.8 %copy-start.1 = (f32[128,128]{1,0:T(8,128)}, f32[128,128]{1,0:T(8,128)S(1)}, u32[]{:S(2)}) copy-start(f32[128,128]{1,0:T(8,128)S(1)} %get-tuple-element.411) | copy-start | bytes 196612
Sparse Core Ops, SparseCore 0:
  75.4 74.0 all-reduce.2
  152.1 130.0 all-reduce.4
where the time goes:
time: 712 us; the launch traced here: 709 us
  waiting for transfers between devices  223 us (31%)
  matrix products  217 us (30%)
  other arithmetic  127 us (18%)
  loops' own time  99.4 us (14%)
  starting transfers between devices  19.3 us (3%)
  between operations  14.3 us (2%)
  local copies, waits for them, and re-layouts  8.73 us (1%)
    psum x1, waiting for transfers between devices, local(): gram = lax.psum(gram, 'lon')  133 us
    dot_general x128, matrix products, column(): resid = col_g - jnp.dot(lower, row_j, precision=lax.Precision.HIGHEST)  105 us
    dot_general x128, matrix products, row_step(): jnp.dot(above, solved, precision=lax.Precision.HIGHEST)  102 us
    another operation x1, loops' own time, chol_upper(): lax.fori_loop(0, order, column, jnp.zeros((order, order), jnp.float32))  94.9 us
    reduce_sum x128, other arithmetic, row_step(): diag = jnp.sum(jnp.where(index == i, row_u, 0.0))  77.7 us
    psum x1, waiting for transfers between devices, local(): gram = lax.psum(partial_gram, 'lat')  74 us
    ppermute x4, starting transfers between devices, extended(): before = lax.ppermute(last, axis, up)  16.3 us
  transfers between devices with their start and end apart: 10, of which 8 were waited for; matrix products, arithmetic and copies ran while one was open for 1% of the time, Pallas kernels for 0%

commit v1 on v0

--- a/solution.py
+++ b/solution.py
@@ -3,6 +3,8 @@
 import jax
 import jax.numpy as jnp
 from jax import lax
+from jax.experimental import pallas as pl
+from jax.experimental.pallas import tpu as pltpu
 from jax.sharding import PartitionSpec as P
 
 
@@ -33,37 +35,60 @@
     return centre + kx[None, :, None, None] * east_west + 0.2 * north_south
 
 
-def chol_upper(gram):
-    order = gram.shape[0]
-    index = jnp.arange(order)
-
-    def column(j, lower):
-        row_j = lax.dynamic_slice_in_dim(lower, j, 1, 0)[0]
-        col_g = lax.dynamic_slice_in_dim(gram, j, 1, 1)[:, 0]
-        resid = col_g - jnp.dot(lower, row_j, precision=lax.Precision.HIGHEST)
-        pivot = jnp.sqrt(jnp.sum(jnp.where(index == j, resid, 0.0)))
-        col_new = jnp.where(index >= j, resid / pivot, 0.0)
-        return lower + col_new[:, None] * (index[None, :] == j).astype(jnp.float32)
-
-    lower = lax.fori_loop(0, order, column, jnp.zeros((order, order), jnp.float32))
-    return lower.T
+N = 128
+B = 8
 
 
-def upper_inverse(upper):
-    order = upper.shape[0]
-    index = jnp.arange(order)
-    ident = jnp.eye(order, dtype=jnp.float32)
+def split3(x):
+    hi = x.astype(jnp.bfloat16)
+    rest = x - hi.astype(jnp.float32)
+    mid = rest.astype(jnp.bfloat16)
+    lo = (rest - mid.astype(jnp.float32)).astype(jnp.bfloat16)
+    return (hi, mid, lo)
 
-    def row_step(step, solved):
-        i = order - 1 - step
-        row_u = lax.dynamic_slice_in_dim(upper, i, 1, 0)[0]
-        diag = jnp.sum(jnp.where(index == i, row_u, 0.0))
-        above = jnp.where(index > i, row_u, 0.0)
-        unit = lax.dynamic_slice_in_dim(ident, i, 1, 0)[0]
-        new_row = (unit - jnp.dot(above, solved, precision=lax.Precision.HIGHEST)) / diag
-        return solved + (index == i).astype(jnp.float32)[:, None] * new_row[None, :]
 
-    return lax.fori_loop(0, order, row_step, jnp.zeros((order, order), jnp.float32))
+def eliminate(w_ref):
+    for b0 in range(0, N, B):
+        rows = [w_ref[b0 + j : b0 + j + 1, :] for j in range(B)]
+        d = {}
+        for i in range(B):
+            for j in range(i, B):
+                d[i, j] = jnp.broadcast_to(rows[i][:, b0 + j : b0 + j + 1], (1, N))
+        for j in range(B):
+            s = lax.rsqrt(d[j, j])
+            u = rows[j] * jnp.concatenate([s, s], axis=1)
+            w_ref[b0 + j : b0 + j + 1, :] = u
+            l = {i: d[j, i] * s for i in range(j + 1, B)}
+            for i in range(j + 1, B):
+                for m in range(i, B):
+                    d[i, m] = d[i, m] - l[i] * l[m]
+                rows[i] = rows[i] - jnp.concatenate([l[i], l[i]], axis=1) * u
+        if b0 + B < N:
+            hi, mid, lo = split3(w_ref[b0 : b0 + B, :])
+            lhs = jnp.concatenate([hi, hi, mid, hi, lo, mid], axis=0)[:, :N]
+            rhs = jnp.concatenate([hi, mid, hi, lo, hi, mid], axis=0)
+            update = lax.dot_general(
+                lhs, rhs, (((0,), (0,)), ((), ())), preferred_element_type=jnp.float32
+            )
+            w_ref[b0 + B :, :] = w_ref[b0 + B :, :] - update[b0 + B :, :]
+
+
+def factor_kernel(g_ref, r_ref, x_ref, w_ref):
+    row = lax.broadcasted_iota(jnp.int32, (N, N), 0)
+    col = lax.broadcasted_iota(jnp.int32, (N, N), 1)
+    w_ref[:, :N] = g_ref[...]
+    w_ref[:, N:] = (row == col).astype(jnp.float32)
+    eliminate(w_ref)
+    r_ref[...] = jnp.where(row <= col, w_ref[:, :N], 0.0)
+    x_ref[...] = jnp.where(row >= col, w_ref[:, N:], 0.0)
+
+
+def factor(gram):
+    return pl.pallas_call(
+        factor_kernel,
+        out_shape=[jax.ShapeDtypeStruct((N, N), jnp.float32)] * 2,
+        scratch_shapes=[pltpu.VMEM((N, 2 * N), jnp.float32)],
+    )(gram)
 
 
 def local(members, background):
@@ -89,10 +114,9 @@
     gram = lax.psum(gram, "lon")
     total_rows = fields * nlat * cols * lax.axis_size("lon")
     gram = gram / total_rows
-    r_factor = chol_upper(gram)
-    inverse = upper_inverse(r_factor)
+    r_factor, inverse_t = factor(gram)
     modes = jnp.dot(
-        matrix, inverse, precision=lax.Precision.HIGHEST, preferred_element_type=jnp.float32
+        matrix, inverse_t.T, precision=lax.Precision.HIGHEST, preferred_element_type=jnp.float32
     )
     return (modes.reshape(fields, rows, cols, width), r_factor)
 

time: 712 us -> 306 us (0.43)
  matrix products: 217 us -> 10 us
  other arithmetic: 127 us -> 23.5 us
  loops' own time: 99.4 us -> 0 us
    dot_general x257 -> x1, matrix products: 215 us -> 8 us  [local(): jnp.dot(matrix, inverse_t.T, precision=lax.Precision.HIGHEST, preferred_e...]
    another operation x2 -> x0, loops' own time: 99.4 us -> none  [the longest x1 94.9 us: chol_upper(): lax.fori_loop(0, order, column, jnp.zeros((order, order), jnp.float32))]
    reduce_sum x128 -> x0, other arithmetic: 77.7 us -> none  [row_step(): diag = jnp.sum(jnp.where(index == i, row_u, 0.0))]
    add x256 -> x0, other arithmetic: 23.7 us -> none  [the longest x128 12.9 us: row_step(): return solved + (index == i).astype(jnp.float32)[:, None] * new_row[None, :]]
where the time goes in v1:
time: 306 us; the launch traced here: 305 us
  waiting for transfers between devices  223 us (73%)
  other arithmetic  23.5 us (8%)
  starting transfers between devices  19.3 us (6%)
  between operations  14.2 us (5%)
  matrix products  10 us (3%)
  local copies, waits for them, and re-layouts  8.56 us (3%)
  Pallas kernels  6.87 us (2%)
    psum x1, waiting for transfers between devices, local(): gram = lax.psum(gram, 'lon')  133 us
    psum x1, waiting for transfers between devices, local(): gram = lax.psum(partial_gram, 'lat')  74 us
    ppermute x4, starting transfers between devices, extended(): before = lax.ppermute(last, axis, up)  16.3 us
    convert_element_type x1, other arithmetic, local(): anomaly = ((final - background.astype(jnp.float32)[:, :, :, None]) * weig...  14 us
    ppermute x4, waiting for transfers between devices, extended(): after = lax.ppermute(leading, axis, down)  9.69 us
    dot_general x1, matrix products, local(): jnp.dot(matrix, inverse_t.T, precision=lax.Precision.HIGHEST, preferred_e...  8 us
    pallas_call x1, Pallas kernels, factor(): pl.pallas_call(factor_kernel, out_shape=[jax.ShapeDtypeStruct((N, N), jnp...  6.87 us
    ppermute x4, waiting for transfers between devices, extended(): before = lax.ppermute(last, axis, up)  6.52 us
  transfers between devices with their start and end apart: 10, of which 8 were waited for; matrix products, arithmetic and copies ran while one was open for 1% of the time, Pallas kernels for 0%

profile of v1, /device:TPU:1, one launch (start us, length us, event | category | flops | bytes accessed | tf_op | source)
XLA Modules:
  0.0 305.5 jit_solution(8644766561012036256)
XLA Ops:
  7.2 2.0 fusion.23
  9.3 4.0 %collective-permute-start = (bf16[3,1,180,128]{3,2,1,0:T(8,128)(2,1)S(1)}, bf16[3,1,180,128]{3,2,1,0:T(8,128)(2,1)S(1)}, u32[]{:S(2)}, u32[]{:S(2)}) collective-permute-start(bf16[3,1,180,128]{3,2,1,0:T(8,128)(2,1)S(1)} %copy.20), channel_id=1, source_target_pairs={{0,1},{1,2},{2,3},{3,4},{4,5},{5,6},{6,7},{8,9},{9,10},{10,11},{11... | collective-permute-start | bytes 414728 | tf_op jit(solution)/shard_map/ppermute | solution.py:18
  13.3 1.3 collective-permute-start.1
  14.6 1.0 collective-permute-done
  15.6 4.3 %constant_dynamic-update-slice_fusion.1 = bf16[3,34,180,128]{3,2,1,0:T(8,128)(2,1)S(1)} fusion(bf16[3,34,180,128]{3,2,1,0:T(8,128)(2,1)S(1)} %constant_dynamic-update-slice_fusion.2, bf16[3,32,180,128]{3,1,2,0:T(8,128)(2,1)} %param.2), kind=kLoop, calls=%fused_computation.37 | loop fusion | bytes 8945664
  20.0 5.1 %collective-permute-start.2 = (bf16[3,34,1,128]{3,2,1,0:T(2,128)(2,1)S(1)}, bf16[3,34,1,128]{3,2,1,0:T(2,128)(2,1)S(1)}, u32[]{:S(2)}, u32[]{:S(2)}) collective-permute-start(bf16[3,34,1,128]{3,2,1,0:T(2,128)(2,1)S(1)} %get-tuple-element.14), channel_id=1, source_target_pairs={{0,8},{8,16},{16,24},{24,32},{32,40},{40,48},{48,56},{56,64},{64,7... | collective-permute-start | bytes 78344 | tf_op jit(solution)/shard_map/ppermute | solution.py:18
  25.2 1.2 collective-permute-done.2
  26.3 3.8 %collective-permute-done.3 = bf16[3,34,1,128]{3,2,1,0:T(2,128)(2,1)S(1)} collective-permute-done((bf16[3,34,1,128]{3,2,1,0:T(2,128)(2,1)S(1)}, bf16[3,34,1,128]{3,2,1,0:T(2,128)(2,1)S(1)}, u32[]{:S(2)}, u32[]{:S(2)}) %collective-permute-start.3) | collective-permute-done | bytes 26144 | tf_op jit(solution)/shard_map/ppermute | solution.py:19
  30.2 2.0 maximum_convert_fusion
  32.1 5.8 %fusion.13 = f32[3,32,180,128]{3,2,1,0:T(8,128)S(1)} fusion(f32[3,34,182,128]{3,2,1,0:T(8,128)S(1)} %maximum_convert_fusion, f32[32]{0:T(128)S(1)} %multiply_add_fusion), kind=kLoop, calls=%fused_computation.22 | loop fusion | flops 19906560 | bytes 53084288 | tf_op jit(solution)/shard_map/add | solution.py:35
  38.0 4.1 %collective-permute-start.4 = (f32[3,1,180,128]{3,2,1,0:T(8,128)S(1)}, f32[3,1,180,128]{3,2,1,0:T(8,128)S(1)}, u32[]{:S(2)}, u32[]{:S(2)}) collective-permute-start(f32[3,1,180,128]{3,2,1,0:T(8,128)S(1)} %get-tuple-element.13), channel_id=1, source_target_pairs={{0,1},{1,2},{2,3},{3,4},{4,5},{5,6},{6,7},{8,9},{9,10},{10,11},{11... | collective-permute-start | bytes 829448 | tf_op jit(solution)/shard_map/ppermute | solution.py:18
  42.1 1.3 collective-permute-start.5
  43.4 4.3 %collective-permute-done.4 = f32[3,1,180,128]{3,2,1,0:T(8,128)S(1)} collective-permute-done((f32[3,1,180,128]{3,2,1,0:T(8,128)S(1)}, f32[3,1,180,128]{3,2,1,0:T(8,128)S(1)}, u32[]{:S(2)}, u32[]{:S(2)}) %collective-permute-start.4) | collective-permute-done | bytes 276512 | tf_op jit(solution)/shard_map/ppermute | solution.py:18
  47.8 4.1 %collective-permute-done.5 = f32[3,1,180,128]{3,2,1,0:T(8,128)S(1)} collective-permute-done((f32[3,1,180,128]{3,2,1,0:T(8,128)S(1)}, f32[3,1,180,128]{3,2,1,0:T(8,128)S(1)}, u32[]{:S(2)}, u32[]{:S(2)}) %collective-permute-start.5) | collective-permute-done | bytes 276512 | tf_op jit(solution)/shard_map/ppermute | solution.py:19
  52.2 3.1 %collective-permute-start.7 = (f32[3,34,1,128]{3,2,1,0:T(1,128)S(1)}, f32[3,34,1,128]{3,2,1,0:T(1,128)S(1)}, u32[]{:S(2)}, u32[]{:S(2)}) collective-permute-start(f32[3,34,1,128]{3,2,1,0:T(1,128)S(1)} %get-tuple-element.11), channel_id=1, source_target_pairs={{0,8},{8,16},{16,24},{24,32},{32,40},{40,48},{48,56},{56,64},{64,7... | collective-permute-start | bytes 156680 | tf_op jit(solution)/shard_map/ppermute | solution.py:18
  55.4 1.7 collective-permute-done.6
  57.1 14.0 %fusion.6 = bf16[3,32,180,128]{3,2,1,0:T(8,128)(2,1)S(1)} fusion(f32[3,32,180,128]{3,2,1,0:T(8,128)S(1)} %fusion.13, f32[3,1,180,128]{3,2,1,0:T(8,128)S(1)} %collective-permute-done.4, f32[3,1,180,128]{3,2,1,0:T(8,128)S(1)} %collective-permute-done.5, f32[3,34,1,128]{3,2,1,0:T(1,128)S(1)} %collective-permute-done.7, ...), kind=kLoop, calls=%fused_computation.7 | loop fusion | flops 44236800 | bytes 13997824 | tf_op jit(solution)/shard_map/convert_element_type | solution.py:108
  71.2 2.1 copy-done
  73.2 2.0 convolution_bitcast_fusion
  75.5 74.0 %all-reduce.3.cloned.1.call-done = f32[128,128]{1,0:T(8,128)} async-done(((f32[128,128]{1,0:T(8,128)}), f32[128,128]{1,0:T(8,128)}) %all-reduce.3.cloned.1.call-update) | async-done | bytes 65552 | tf_op jit(solution)/shard_map/psum | solution.py:113
  149.5 132.7 %all-reduce.5.cloned.1.call-done = f32[128,128]{1,0:T(8,128)} async-done(((f32[128,128]{1,0:T(8,128)}), f32[128,128]{1,0:T(8,128)}) %all-reduce.5.cloned.1.call-update) | async-done | bytes 65552 | tf_op jit(solution)/shard_map/psum | solution.py:114
  282.3 1.5 broadcast_multiply_fusion.g_ref
  283.7 6.9 %shard_map.41 = (f32[128,128]{1,0:T(8,128)}, f32[128,128]{1,0:T(8,128)}) custom-call(f32[128,128]{1,0:T(8,128)} %broadcast_multiply_fusion.g_ref), custom_call_target="tpu_custom_call" | custom-call | tf_op jit(solution)/shard_map/pallas_call | solution.py:87
  290.6 8.0 %fusion.17 = f32[3,32,180,128]{3,1,2,0:T(8,128)} fusion(bf16[3,32,180,128]{3,2,1,0:T(8,128)(2,1)} %copy-done, f32[128,128]{1,0:T(8,128)} %get-tuple-element.4), kind=kOutput, calls=%fused_computation.28 | convolution fusion | flops 3397386240 | bytes 13336576 | tf_op jit(solution)/shard_map/dot_general | solution.py:118
  (21 shorter events, 0.9 us)
Async XLA Ops:
  7.2 142.4 %all-reduce.3.cloned.1.call-start = ((), (), s32[]{:S(2)}) async-start(), calls=%async_computation | async-start | bytes 131072 | tf_op jit(solution)/shard_map/psum | solution.py:113
  9.3 6.3 %collective-permute-start = (bf16[3,1,180,128]{3,2,1,0:T(8,128)(2,1)S(1)}, bf16[3,1,180,128]{3,2,1,0:T(8,128)(2,1)S(1)}, u32[]{:S(2)}, u32[]{:S(2)}) collective-permute-start(bf16[3,1,180,128]{3,2,1,0:T(8,128)(2,1)S(1)} %copy.20), channel_id=1, source_target_pairs={{0,1},{1,2},{2,3},{3,4},{4,5},{5,6},{6,7},{8,9},{9,10},{10,11},{11... | collective-permute-start | bytes 414728 | tf_op jit(solution)/shard_map/ppermute | solution.py:18
  13.3 6.6 %collective-permute-start.1 = (bf16[3,1,180,128]{3,2,1,0:T(8,128)(2,1)S(1)}, bf16[3,1,180,128]{3,2,1,0:T(8,128)(2,1)S(1)}, u32[]{:S(2)}, u32[]{:S(2)}) collective-permute-start(bf16[3,1,180,128]{3,2,1,0:T(8,128)(2,1)S(1)} %copy.21), channel_id=1, source_target_pairs={{1,0},{2,1},{3,2},{4,3},{5,4},{6,5},{7,6},{9,8},{10,9},{11,10},{12... | collective-permute-start | bytes 414728 | tf_op jit(solution)/shard_map/ppermute | solution.py:19
  20.0 6.3 %collective-permute-start.2 = (bf16[3,34,1,128]{3,2,1,0:T(2,128)(2,1)S(1)}, bf16[3,34,1,128]{3,2,1,0:T(2,128)(2,1)S(1)}, u32[]{:S(2)}, u32[]{:S(2)}) collective-permute-start(bf16[3,34,1,128]{3,2,1,0:T(2,128)(2,1)S(1)} %get-tuple-element.14), channel_id=1, source_target_pairs={{0,8},{8,16},{16,24},{24,32},{32,40},{40,48},{48,56},{56,64},{64,7... | collective-permute-start | bytes 78344 | tf_op jit(solution)/shard_map/ppermute | solution.py:18
  25.1 5.1 %collective-permute-start.3 = (bf16[3,34,1,128]{3,2,1,0:T(2,128)(2,1)S(1)}, bf16[3,34,1,128]{3,2,1,0:T(2,128)(2,1)S(1)}, u32[]{:S(2)}, u32[]{:S(2)}) collective-permute-start(bf16[3,34,1,128]{3,2,1,0:T(2,128)(2,1)S(1)} %get-tuple-element.15), channel_id=1, source_target_pairs={{8,0},{16,8},{24,16},{32,24},{40,32},{48,40},{56,48},{64,56},{72,6... | collective-permute-start | bytes 78344 | tf_op jit(solution)/shard_map/ppermute | solution.py:19
  38.0 17.4 %copy-start.1 = (bf16[3,32,180]{2,1,0:T(8,128)(2,1)S(1)}, bf16[3,32,180]{2,1,0:T(8,128)(2,1)}, u32[]{:S(2)}) copy-start(bf16[3,32,180]{2,1,0:T(8,128)(2,1)} %param.3) | copy-start | bytes 103684
  38.0 9.8 %collective-permute-start.4 = (f32[3,1,180,128]{3,2,1,0:T(8,128)S(1)}, f32[3,1,180,128]{3,2,1,0:T(8,128)S(1)}, u32[]{:S(2)}, u32[]{:S(2)}) collective-permute-start(f32[3,1,180,128]{3,2,1,0:T(8,128)S(1)} %get-tuple-element.13), channel_id=1, source_target_pairs={{0,1},{1,2},{2,3},{3,4},{4,5},{5,6},{6,7},{8,9},{9,10},{10,11},{11... | collective-permute-start | bytes 829448 | tf_op jit(solution)/shard_map/ppermute | solution.py:18
  42.1 9.7 %collective-permute-start.5 = (f32[3,1,180,128]{3,2,1,0:T(8,128)S(1)}, f32[3,1,180,128]{3,2,1,0:T(8,128)S(1)}, u32[]{:S(2)}, u32[]{:S(2)}) collective-permute-start(f32[3,1,180,128]{3,2,1,0:T(8,128)S(1)} %get-tuple-element.12), channel_id=1, source_target_pairs={{1,0},{2,1},{3,2},{4,3},{5,4},{6,5},{7,6},{9,8},{10,9},{11,10},{12... | collective-permute-start | bytes 829448 | tf_op jit(solution)/shard_map/ppermute | solution.py:19
  52.0 5.1 %collective-permute-start.6 = (f32[3,34,1,128]{3,2,1,0:T(1,128)S(1)}, f32[3,34,1,128]{3,2,1,0:T(1,128)S(1)}, u32[]{:S(2)}, u32[]{:S(2)}) collective-permute-start(f32[3,34,1,128]{3,2,1,0:T(1,128)S(1)} %get-tuple-element.10), channel_id=1, source_target_pairs={{8,0},{16,8},{24,16},{32,24},{40,32},{48,40},{56,48},{64,56},{72,6... | collective-permute-start | bytes 156680 | tf_op jit(solution)/shard_map/ppermute | solution.py:19
  52.2 5.0 %collective-permute-start.7 = (f32[3,34,1,128]{3,2,1,0:T(1,128)S(1)}, f32[3,34,1,128]{3,2,1,0:T(1,128)S(1)}, u32[]{:S(2)}, u32[]{:S(2)}) collective-permute-start(f32[3,34,1,128]{3,2,1,0:T(1,128)S(1)} %get-tuple-element.11), channel_id=1, source_target_pairs={{0,8},{8,16},{16,24},{24,32},{32,40},{40,48},{48,56},{56,64},{64,7... | collective-permute-start | bytes 156680 | tf_op jit(solution)/shard_map/ppermute | solution.py:18
  71.2 2.1 copy-start
  75.3 207.0 %all-reduce.5.cloned.1.call-start = ((), (), s32[]{:S(2)}) async-start(), calls=%async_computation.1 | async-start | bytes 131072 | tf_op jit(solution)/shard_map/psum | solution.py:114
Sparse Core Ops, SparseCore 0:
  75.4 74.0 all-reduce.2
  152.1 130.0 all-reduce.4

commit v2 on v1

v2 whole, which is shorter than its diff:
```python
import functools
import math

import jax
import jax.numpy as jnp
import numpy as np
from jax import lax
from jax.experimental import pallas as pl
from jax.experimental.pallas import tpu as pltpu
from jax.sharding import PartitionSpec as P

N = 128
B = 8
F, ROWS, COLS = 3, 32, 180
LEFT = 16
PAD = 208
PADS = 216
WIDE = 192
CHUNK = 64
MESH = pl.DeviceIdType.MESH


def split3(x):
    hi = x.astype(jnp.bfloat16)
    rest = x - hi.astype(jnp.float32)
    mid = rest.astype(jnp.bfloat16)
    lo = (rest - mid.astype(jnp.float32)).astype(jnp.bfloat16)
    return (hi, mid, lo)


def eliminate(w_ref):
    for b0 in range(0, N, B):
        rows = [w_ref[b0 + j : b0 + j + 1, :] for j in range(B)]
        d = {}
        for i in range(B):
            for j in range(i, B):
                d[i, j] = jnp.broadcast_to(rows[i][:, b0 + j : b0 + j + 1], (1, N))
        for j in range(B):
            s = lax.rsqrt(d[j, j])
            u = rows[j] * jnp.concatenate([s, s], axis=1)
            w_ref[b0 + j : b0 + j + 1, :] = u
            l = {i: d[j, i] * s for i in range(j + 1, B)}
            for i in range(j + 1, B):
                for m in range(i, B):
                    d[i, m] = d[i, m] - l[i] * l[m]
                rows[i] = rows[i] - jnp.concatenate([l[i], l[i]], axis=1) * u
        if b0 + B < N:
            hi, mid, lo = split3(w_ref[b0 : b0 + B, :])
            lhs = jnp.concatenate([hi, hi, mid, hi, lo, mid], axis=0)[:, :N]
            rhs = jnp.concatenate([hi, mid, hi, lo, hi, mid], axis=0)
            update = lax.dot_general(
                lhs, rhs, (((0,), (0,)), ((), ())), preferred_element_type=jnp.float32
            )
            w_ref[b0 + B :, :] = w_ref[b0 + B :, :] - update[b0 + B :, :]


def row_table(nlat):
    phi = (0.125 * (np.arange(-1, nlat + 1) + 0.5) - 0.0625 * nlat) * (math.pi / 180.0)
    kx = 0.05 + 0.2 * (1.0 - np.cos(phi))
    return np.stack([3.0 - 10.0 * kx, 5.0 * kx, 0.04 * np.sqrt(np.cos(phi))]).astype(np.float32)


def basis_kernel(
    n_lon, n_lat, total,
    m_ref, bg_ref, coef_ref, a_out, r_ref, w_out,
    ub, fu, s1, a_buf, bt, bgp, gram, part, got1, got2, work,
    load_sem, hs_sem, hr_sem, s1_sem, r1_sem, s2_sem, r2_sem, s3_sem, r3_sem, out_sem,
):
    lon, lat = lax.axis_index("lon"), lax.axis_index("lat")
    first = lat * ROWS + 1

    loads = [
        pltpu.make_async_copy(m_ref.at[f], ub.at[f, 2 : 2 + ROWS, LEFT : LEFT + COLS, :], load_sem.at[f])
        for f in range(F)
    ]
    for copy in loads:
        copy.start()

    east, west = lax.rem(lon + 1, n_lon), lax.rem(lon + n_lon - 1, n_lon)
    north, south = lax.rem(lat + n_lat - 1, n_lat), lax.rem(lat + 1, n_lat)

    barrier = pltpu.get_barrier_semaphore()
    for d in range(1, n_lon):
        pl.semaphore_signal(barrier, inc=1, device_id={"lon": lax.rem(lon + d, n_lon), "lat": lat}, device_id_type=MESH)
    for d in range(1, n_lat):
        pl.semaphore_signal(barrier, inc=1, device_id={"lon": lon, "lat": lax.rem(lat + d, n_lat)}, device_id_type=MESH)
    for a in (east, west):
        for b in (north, south):
            pl.semaphore_signal(barrier, inc=1, device_id={"lon": a, "lat": b}, device_id_type=MESH)
    pl.semaphore_wait(barrier, n_lon + n_lat + 2)

    lo_c, hi_c = LEFT - 2, LEFT + COLS
    end_r = 2 + ROWS
    rows = pl.ds(2, ROWS)
    cols = pl.ds(LEFT, COLS)
    plan = [
        (slice(ROWS - 2, ROWS), slice(0, COLS), pl.ds(0, 2), cols, lon, south),
        (slice(0, 2), slice(0, COLS), pl.ds(end_r, 2), cols, lon, north),
        (slice(0, ROWS), slice(COLS - 2, COLS), rows, pl.ds(lo_c, 2), east, lat),
        (slice(0, ROWS), slice(0, 2), rows, pl.ds(hi_c, 2), west, lat),
        (slice(ROWS - 1, ROWS), slice(COLS - 2, COLS), pl.ds(1, 1), pl.ds(lo_c, 2), east, south),
        (slice(ROWS - 1, ROWS), slice(0, 2), pl.ds(1, 1), pl.ds(hi_c, 2), west, south),
        (slice(0, 1), slice(COLS - 2, COLS), pl.ds(end_r, 1), pl.ds(lo_c, 2), east, north),
        (slice(0, 1), slice(0, 2), pl.ds(end_r, 1), pl.ds(hi_c, 2), west, north),
    ]
    halos = [
        pltpu.make_async_remote_copy(
            src_ref=m_ref.at[:, sr, sc, :],
            dst_ref=ub.at[:, dr, dc, :],
            send_sem=hs_sem.at[i],
            recv_sem=hr_sem.at[i],
            device_id={"lon": a, "lat": b},
            device_id_type=MESH,
        )
        for i, (sr, sc, dr, dc, a, b) in enumerate(plan)
    ]
    for i in (2, 3, 0, 1, 4, 5, 6, 7):
        halos[i].start()

    bgp[...] = jnp.zeros_like(bgp)
    for f in range(F):
        bgp[0:ROWS, 0:COLS] = bg_ref[f].astype(jnp.float32) * 25.0
        for h in range(2):
            bt[f, h * N : (h + 1) * N, :] = bgp[:, h * N : (h + 1) * N].T
    gram[...] = jnp.zeros_like(gram)
    keep = lax.broadcasted_iota(jnp.int32, (CHUNK, N), 0) < COLS - 2 * CHUNK

    def widen(f, i):
        fu[f, i] = ub[f, i].astype(jnp.float32)

    def first_pass(f, r, above=None, scale=None):
        ca, ck = coef_ref[0, first + r], coef_ref[1, first + r]
        for c in range(8, 8 + WIDE, CHUNK):
            centre = fu[f, r + 2, c : c + CHUNK]
            sides = fu[f, r + 2, c - 1 : c - 1 + CHUNK] + fu[f, r + 2, c + 1 : c + 1 + CHUNK]
            up, down = fu[f, r + 1, c : c + CHUNK], fu[f, r + 3, c : c + CHUNK]
            if above is not None:
                up, down = above(up, down)
            out = ca * centre + ck * sides + (up + down)
            if scale is not None:
                out = out * scale
            s1[f, r + 1, c : c + CHUNK] = out

    def second_pass(f, r):
        ca, ck, cw = coef_ref[0, first + r], coef_ref[1, first + r], coef_ref[2, first + r]
        for h in range(WIDE // CHUNK):
            c = LEFT + h * CHUNK
            centre = s1[f, r + 1, c : c + CHUNK]
            sides = s1[f, r + 1, c - 1 : c - 1 + CHUNK] + s1[f, r + 1, c + 1 : c + 1 + CHUNK]
            up, down = s1[f, r, c : c + CHUNK], s1[f, r + 2, c : c + CHUNK]
            ground = jnp.broadcast_to(bt[f, h * CHUNK : (h + 1) * CHUNK, r : r + 1], (CHUNK, N))
            out = (ca * centre + ck * sides + (up + down) - ground) * cw
            if h == 2:
                out = jnp.where(keep, out, 0.0)
            a_buf[f, r, h * CHUNK : (h + 1) * CHUNK] = out.astype(jnp.bfloat16)

    def add_gram(f, r, n):
        block = a_buf[f, r : r + n].reshape(n * WIDE, N)
        gram[...] += lax.dot_general(block, block, (((0,), (0,)), ((), ())), preferred_element_type=jnp.float32)

    halos[2].wait()
    halos[3].wait()
    for f in range(F):
        loads[f].wait()

    def interior(f, carry):
        def w(i, c):
            widen(f, i)
            return c

        lax.fori_loop(2, 2 + ROWS, w, 0)

        def p1(r, c):
            first_pass(f, r)
            return c

        lax.fori_loop(1, ROWS - 1, p1, 0)
        for r0 in range(2, ROWS - 2, 7):
            for r in range(r0, r0 + 7):
                second_pass(f, r)
            add_gram(f, r0, 7)
        return carry

    lax.fori_loop(0, F, interior, 0)

    for i in (0, 1, 4, 5, 6, 7):
        halos[i].wait()
    top = jnp.where(lat > 0, 1.0, 0.0).astype(jnp.float32)
    bottom = jnp.where(lat < n_lat - 1, 1.0, 0.0).astype(jnp.float32)

    def border(f, carry):
        for i in (0, 1, ROWS + 2, ROWS + 3):
            widen(f, i)
        first_pass(f, -1, scale=top)
        first_pass(f, 0, above=lambda up, down: (up * top, down))
        first_pass(f, ROWS - 1, above=lambda up, down: (up, down * bottom))
        first_pass(f, ROWS, scale=bottom)
        for r0 in (0, ROWS - 2):
            for r in (r0, r0 + 1):
                second_pass(f, r)
            add_gram(f, r0, 2)
        return carry

    lax.fori_loop(0, F, border, 0)
    store = pltpu.make_async_copy(a_buf, a_out, out_sem)
    store.start()

    size = N // n_lon
    scatter = []
    for d in range(1, n_lon):
        peer = lax.rem(lon + d, n_lon)
        copy = pltpu.make_async_remote_copy(
            src_ref=gram.at[pl.ds(pl.multiple_of(peer * size, size), size), :],
            dst_ref=got1.at[n_lon - 1 - d],
            send_sem=s1_sem.at[d],
            recv_sem=r1_sem.at[d],
            device_id={"lon": peer, "lat": lat},
            device_id_type=MESH,
        )
        copy.start()
        scatter.append(copy)
    mine = pl.ds(pl.multiple_of(lon * size, size), size)
    acc = gram[mine, :]
    for copy in scatter:
        copy.wait()
    for d in range(n_lon - 1):
        acc = acc + got1[d]
    part[...] = acc
    exchange = []
    for d in range(1, n_lat):
        copy = pltpu.make_async_remote_copy(
            src_ref=part,
            dst_ref=got2.at[lat],
            send_sem=s2_sem.at[d],
            recv_sem=r2_sem.at[d],
            device_id={"lon": lon, "lat": lax.rem(lat + d, n_lat)},
            device_id_type=MESH,
        )
        copy.start()
        exchange.append(copy)
    got2[lat] = acc
    for copy in exchange:
        copy.wait()
    acc = got2[0]
    for d in range(1, n_lat):
        acc = acc + got2[d]
    work[mine, 0:N] = acc / total
    gather = []
    for d in range(1, n_lon):
        copy = pltpu.make_async_remote_copy(
            src_ref=work.at[mine, 0:N],
            dst_ref=work.at[mine, 0:N],
            send_sem=s3_sem.at[d],
            recv_sem=r3_sem.at[d],
            device_id={"lon": lax.rem(lon + d, n_lon), "lat": lat},
            device_id_type=MESH,
        )
        copy.start()
        gather.append(copy)
    row = lax.broadcasted_iota(jnp.int32, (N, N), 0)
    col = lax.broadcasted_iota(jnp.int32, (N, N), 1)
    work[:, N:] = (row == col).astype(jnp.float32)
    for copy in gather:
        copy.wait()

    eliminate(work)
    r_ref[...] = jnp.where(row <= col, work[:, :N], 0.0)
    inverse = jnp.where(row >= col, work[:, N:], 0.0).T
    hi, mid, lo = split3(inverse)
    w_out[0:N, 0:N] = hi
    w_out[N:, 0:N] = mid
    w_out[0:N, N:] = lo
    w_out[N:, N:] = jnp.zeros((N, N), jnp.bfloat16)
    store.wait()


def modes_kernel(slabs, a_ref, w_ref, o_ref):
    for s in range(slabs):
        a = a_ref[s]
        out = jnp.dot(jnp.concatenate([a, a], axis=1), w_ref[...], preferred_element_type=jnp.float32)
        o_ref[s] = (out[:, :N] + out[:, N:])[:COLS]


def local(n_lon, n_lat, members, background):
    coefs = jnp.asarray(row_table(n_lat * ROWS))
    size = N // n_lon
    vmem, anywhere = pl.BlockSpec(memory_space=pltpu.VMEM), pl.BlockSpec(memory_space=pl.ANY)
    dma = pltpu.SemaphoreType.DMA
    anomaly, r_factor, weights = pl.pallas_call(
        functools.partial(basis_kernel, n_lon, n_lat, float(F * ROWS * COLS * n_lon * n_lat)),
        out_shape=[
            jax.ShapeDtypeStruct((F, ROWS, WIDE, N), jnp.bfloat16),
            jax.ShapeDtypeStruct((N, N), jnp.float32),
            jax.ShapeDtypeStruct((2 * N, 2 * N), jnp.bfloat16),
        ],
        in_specs=[anywhere, vmem, pl.BlockSpec(memory_space=pltpu.SMEM)],
        out_specs=[anywhere, vmem, vmem],
        scratch_shapes=[
            pltpu.VMEM((F, ROWS + 4, PAD, N), jnp.bfloat16),
            pltpu.VMEM((F, ROWS + 4, PAD, N), jnp.float32),
            pltpu.VMEM((F, ROWS + 2, PADS, N), jnp.float32),
            pltpu.VMEM((F, ROWS, WIDE, N), jnp.bfloat16),
            pltpu.VMEM((F, 2 * N, N), jnp.float32),
            pltpu.VMEM((N, 2 * N), jnp.float32),
            pltpu.VMEM((N, N), jnp.float32),
            pltpu.VMEM((size, N), jnp.float32),
            pltpu.VMEM((n_lon - 1, size, N), jnp.float32),
            pltpu.VMEM((n_lat, size, N), jnp.float32),
            pltpu.VMEM((N, 2 * N), jnp.float32),
            dma((F,)),
            dma((8,)),
            dma((8,)),
            dma((n_lon,)),
            dma((n_lon,)),
            dma((n_lat,)),
            dma((n_lat,)),
            dma((n_lon,)),
            dma((n_lon,)),
            dma(()),
        ],
        compiler_params=pltpu.CompilerParams(
            collective_id=0, has_side_effects=True, vmem_limit_bytes=48 * 1024 * 1024
        ),
        name="basis",
    )(members, background, coefs)
    slabs = 12
    modes = pl.pallas_call(
        functools.partial(modes_kernel, slabs),
        grid=(F * ROWS // slabs,),
        out_shape=jax.ShapeDtypeStruct((F * ROWS, COLS, N), jnp.float32),
        in_specs=[
            pl.BlockSpec((slabs, WIDE, N), lambda i: (i, 0, 0)),
            pl.BlockSpec((2 * N, 2 * N), lambda i: (0, 0)),
        ],
        out_specs=pl.BlockSpec((slabs, COLS, N), lambda i: (i, 0, 0)),
        compiler_params=pltpu.CompilerParams(vmem_limit_bytes=32 * 1024 * 1024),
        name="modes",
    )(anomaly.reshape(F * ROWS, WIDE, N), weights)
    return (modes.reshape(F, ROWS, COLS, N), r_factor)


def solution(mesh):
    return jax.shard_map(
        functools.partial(local, mesh.shape["lon"], mesh.shape["lat"]),
        mesh=mesh,
        in_specs=(P(None, "lat", "lon", None), P(None, "lat", "lon")),
        out_specs=(P(None, "lat", "lon", None), P()),
        check_vma=False,
    )
```

time: 306 us -> 66 us (0.22)
  waiting for transfers between devices: 223 us -> 0 us
  Pallas kernels: 6.87 us -> 53.1 us
  other arithmetic: 23.5 us -> 0 us
  starting transfers between devices: 19.3 us -> 0 us
  between operations: 14.2 us -> 0.69 us
  matrix products: 10 us -> 0 us
  local copies, waits for them, and re-layouts: 8.56 us -> 12 us
    psum x2 -> x0, waiting for transfers between devices: 207 us -> none  [the longest x1 133 us: local(): gram = lax.psum(gram, 'lon')]
    pallas_call x1 -> x2, Pallas kernels: 6.87 us -> 53.1 us  [the longest x1 49.2 us: local(): pl.pallas_call(functools.partial(basis_kernel, n_lon, n_lat, float(F * RO...]
    ppermute x8 -> x0, starting transfers between devices: 19.1 us -> none  [the longest x4 16.3 us: extended(): before = lax.ppermute(last, axis, up)]
    ppermute x8 -> x0, waiting for transfers between devices: 16.2 us -> none  [the longest x4 9.69 us: extended(): after = lax.ppermute(leading, axis, down)]
    convert_element_type x3 -> x0, other arithmetic: 16 us -> none  [the longest x1 14 us: local(): anomaly = ((final - background.astype(jnp.float32)[:, :, :, None]) * weig...]
    dot_general x2 -> x0, matrix products: 10 us -> none  [the longest x1 8 us: local(): jnp.dot(matrix, inverse_t.T, precision=lax.Precision.HIGHEST, preferred_e...]
    add x2 -> x0, other arithmetic: 5.89 us -> none  [the longest x1 5.84 us: smooth_pass(): return centre + kx[None, :, None, None] * east_west + 0.2 * north_south]
    unnamed x8 -> x9, local copies, waits for them, and re-layouts: 6.38 us -> 12 us
  transfers between devices with their start and end apart: 10 -> 0, of which waited for: 8 -> 0; matrix products, arithmetic and copies ran while one was open for 1% -> 0% of each run, Pallas kernels for 0% -> 0%
where the time goes in v2:
time: 66 us; the launch traced here: 65.8 us
  Pallas kernels  53.1 us (80%)
  local copies, waits for them, and re-layouts  12 us (18%)
  between operations  0.69 us (1%)
    pallas_call x1, Pallas kernels, local(): pl.pallas_call(functools.partial(basis_kernel, n_lon, n_lat, float(F * RO...  49.2 us
    unnamed x9, local copies, waits for them, and re-layouts  12 us
    pallas_call x1, Pallas kernels, local(): pl.pallas_call(functools.partial(modes_kernel, slabs), grid=(F * ROWS //...  3.85 us

profile of v2, /device:TPU:1, one launch (start us, length us, event | category | flops | bytes accessed | tf_op | source)
XLA Modules:
  0.0 65.8 jit_solution(9566965411837469522)
XLA Ops:
  0.6 0.0 copy-start.2
  0.6 0.0 copy-start.1
  0.7 4.0 %copy.5.m_ref = bf16[3,32,180,128]{3,2,1,0:T(8,128)(2,1)S(1)} copy(bf16[3,32,180,128]{3,1,2,0:T(8,128)(2,1)} %param.3) | data formatting | bytes 8847360 | tf_op args[0]
  4.6 0.0 copy-done.2
  4.7 0.0 copy-done.1
  4.7 49.2 %basis.1 = (bf16[3,32,192,128]{3,2,1,0:T(8,128)(2,1)}, f32[128,128]{1,0:T(8,128)S(1)}, bf16[256,256]{1,0:T(8,128)(2,1)S(1)}) custom-call(bf16[3,32,180,128]{3,2,1,0:T(8,128)(2,1)S(1)} %copy.5.m_ref, bf16[3,32,180]{2,1,0:T(8,128)(2,1)S(1)} %copy-done.1, f32[3,258]{1,0:T(4,128)S(1)} %copy-done.2), custom_call_target="tpu_custom_call" | custom-call | tf_op jit(solution)/shard_map/basis/pallas_call | solution.py:289
  53.9 0.0 copy-start
  53.9 2.3 %copy-done = bf16[3,32,192,128]{3,2,1,0:T(8,128)(2,1)S(1)} copy-done((bf16[3,32,192,128]{3,2,1,0:T(8,128)(2,1)S(1)}, bf16[3,32,192,128]{3,2,1,0:T(8,128)(2,1)}, u32[]{:S(2)}) %copy-start) | copy-done | bytes 4718616
  56.2 3.8 %modes.1 = f32[96,180,128]{2,1,0:T(8,128)S(1)} custom-call(bf16[96,192,128]{2,1,0:T(8,128)(2,1)S(1)} %bitcast.3, bf16[256,256]{1,0:T(8,128)(2,1)S(1)} %get-tuple-element.6.w_ref), custom_call_target="tpu_custom_call" | custom-call | tf_op jit(solution)/shard_map/modes/pallas_call | solution.py:327
  60.1 5.1 %copy.6 = f32[3,32,180,128]{3,1,2,0:T(8,128)} copy(f32[3,32,180,128]{3,2,1,0:T(8,128)S(1)} %bitcast.2) | data formatting | bytes 17694720
  65.2 0.6 copy.8
Async XLA Ops:
  0.6 4.0 %copy-start.2 = (f32[3,258]{1,0:T(4,128)S(1)}, f32[3,258]{1,0:T(4,128)}, u32[]{:S(2)}) copy-start(f32[3,258]{1,0:T(4,128)} %constant.2.clone.coef_ref) | copy-start | bytes 9292
  0.6 4.0 %copy-start.1 = (bf16[3,32,180]{2,1,0:T(8,128)(2,1)S(1)}, bf16[3,32,180]{2,1,0:T(8,128)(2,1)}, u32[]{:S(2)}) copy-start(bf16[3,32,180]{2,1,0:T(8,128)(2,1)} %bg_ref.1) | copy-start | bytes 103684
  53.9 2.3 %copy-start = (bf16[3,32,192,128]{3,2,1,0:T(8,128)(2,1)S(1)}, bf16[3,32,192,128]{3,2,1,0:T(8,128)(2,1)}, u32[]{:S(2)}) copy-start(bf16[3,32,192,128]{3,2,1,0:T(8,128)(2,1)} %get-tuple-element.5) | copy-start | bytes 14155780

commit v3 on v1

v3 whole, which is shorter than its diff:
```python
import functools
import math

import jax
import jax.numpy as jnp
import numpy as np
from jax import lax
from jax.experimental import pallas as pl
from jax.experimental.pallas import tpu as pltpu
from jax.sharding import PartitionSpec as P

N = 128
B = 8
F, ROWS, COLS = 3, 32, 180
GROUP = 60
WIN = 40
PACK = 48
MESH = pl.DeviceIdType.MESH


def split3(x):
    hi = x.astype(jnp.bfloat16)
    rest = x - hi.astype(jnp.float32)
    mid = rest.astype(jnp.bfloat16)
    lo = (rest - mid.astype(jnp.float32)).astype(jnp.bfloat16)
    return (hi, mid, lo)


def eliminate(w_ref):
    for b0 in range(0, N, B):
        rows = [w_ref[b0 + j : b0 + j + 1, :] for j in range(B)]
        d = {}
        for i in range(B):
            for j in range(i, B):
                d[i, j] = jnp.broadcast_to(rows[i][:, b0 + j : b0 + j + 1], (1, N))
        for j in range(B):
            s = lax.rsqrt(d[j, j])
            u = rows[j] * jnp.concatenate([s, s], axis=1)
            w_ref[b0 + j : b0 + j + 1, :] = u
            l = {i: d[j, i] * s for i in range(j + 1, B)}
            for i in range(j + 1, B):
                for m in range(i, B):
                    d[i, m] = d[i, m] - l[i] * l[m]
                rows[i] = rows[i] - jnp.concatenate([l[i], l[i]], axis=1) * u
        if b0 + B < N:
            hi, mid, lo = split3(w_ref[b0 : b0 + B, :])
            lhs = jnp.concatenate([hi, hi, mid, hi, lo, mid], axis=0)[:, :N]
            rhs = jnp.concatenate([hi, mid, hi, lo, hi, mid], axis=0)
            update = lax.dot_general(
                lhs, rhs, (((0,), (0,)), ((), ())), preferred_element_type=jnp.float32
            )
            w_ref[b0 + B :, :] = w_ref[b0 + B :, :] - update[b0 + B :, :]


def row_table(nlat):
    glob = np.arange(nlat // ROWS)[:, None] * ROWS + np.arange(-1, WIN - 1)[None, :]

    def of(rows):
        phi = (0.125 * (rows + 0.5) - 0.0625 * nlat) * (math.pi / 180.0)
        return 0.05 + 0.2 * (1.0 - np.cos(phi)), np.sqrt(np.cos(phi))

    kx, _ = of(glob)
    _, weight = of(glob + 1)
    inside = ((glob >= 0) & (glob < nlat)).astype(np.float64)
    table = np.stack([3.0 - 10.0 * kx, 5.0 * kx, inside, 0.04 * weight], axis=1)
    return table.astype(np.float32)


def basis_kernel(
    n_lon, n_lat, total, remote, phases,
    m_ref, bg_ref, coef_ref, a_out, r_ref, w_out,
    ub, fu, s1, a_buf, bt, cf, gram, part, got1, got2, work, bgv,
    load_sem, small_sem, hs_sem, hr_sem, s1_sem, r1_sem, s2_sem, r2_sem, s3_sem, r3_sem, out_sem,
):
    if remote:
        lon, lat = lax.axis_index("lon"), lax.axis_index("lat")
    else:
        lon, lat = 0, 0
    loads = [
        pltpu.make_async_copy(m_ref.at[f], ub.at[f, pl.ds(2, COLS), pl.ds(2, ROWS), :], load_sem.at[f])
        for f in range(F)
    ]
    for copy in loads:
        if "nodma" not in phases:
            copy.start()
    small = [
        pltpu.make_async_copy(bg_ref, bgv, small_sem.at[0]),
        pltpu.make_async_copy(coef_ref.at[lat], cf, small_sem.at[1]),
    ]
    for copy in small:
        copy.start()
    not_first, not_last = lat > 0, lat < n_lat - 1
    halos = []
    if remote:
        east, west = lax.rem(lon + 1, n_lon), lax.rem(lon + n_lon - 1, n_lon)
        north, south = lax.rem(lat + n_lat - 1, n_lat), lax.rem(lat + 1, n_lat)

        barrier = pltpu.get_barrier_semaphore()
        for a in (east, west):
            for b in (north, south):
                pl.semaphore_signal(barrier, inc=1, device_id={"lon": a, "lat": b}, device_id_type=MESH)
        for d in range(1, n_lat):
            pl.semaphore_signal(barrier, inc=1, device_id={"lon": lon, "lat": lax.rem(lat + d, n_lat)}, device_id_type=MESH)
        for d in range(1, n_lon):
            pl.semaphore_signal(barrier, inc=1, device_id={"lon": lax.rem(lon + d, n_lon), "lat": lat}, device_id_type=MESH)
        pl.semaphore_wait(barrier, n_lon + n_lat + 2)

        end = 2 + ROWS
        rows, cols = pl.ds(2, ROWS), pl.ds(2, COLS)
        top, bottom, left, right = pl.ds(0, 2), pl.ds(end, 2), pl.ds(0, 2), pl.ds(2 + COLS, 2)
        left1, right1 = pl.ds(1, 1), pl.ds(2 + COLS, 1)
        plan = [
            (pl.ds(COLS - 2, 2), pl.ds(0, ROWS), left, rows, east, lat, None, None),
            (pl.ds(0, 2), pl.ds(0, ROWS), right, rows, west, lat, None, None),
            (pl.ds(0, COLS), pl.ds(ROWS - 2, 2), cols, top, lon, south, not_last, not_first),
            (pl.ds(0, COLS), pl.ds(0, 2), cols, bottom, lon, north, not_first, not_last),
            (pl.ds(COLS - 1, 1), pl.ds(ROWS - 2, 2), left1, top, east, south, not_last, not_first),
            (pl.ds(0, 1), pl.ds(ROWS - 2, 2), right1, top, west, south, not_last, not_first),
            (pl.ds(COLS - 1, 1), pl.ds(0, 2), left1, bottom, east, north, not_first, not_last),
            (pl.ds(0, 1), pl.ds(0, 2), right1, bottom, west, north, not_first, not_last),
        ]
        for f in range(F):
            for i, (sc, sr, dc, dr, a, b, send, receive) in enumerate(plan):
                copy = pltpu.make_async_remote_copy(
                    src_ref=m_ref.at[f, sc, sr, :],
                    dst_ref=ub.at[f, dc, dr, :],
                    send_sem=hs_sem.at[f, i],
                    recv_sem=hr_sem.at[f, i],
                    device_id={"lon": a, "lat": b},
                    device_id_type=MESH,
                )
                halos.append((f, copy, send, receive))
                if send is None:
                    copy.start()
                else:
                    pl.when(send)(copy.start)

    def finish(f):
        for g, copy, send, receive in halos:
            if g == f:
                if send is None:
                    copy.wait()
                else:
                    pl.when(receive)(copy.wait_recv)
                    pl.when(send)(copy.wait_send)

    def clear(at):
        def body(c, carry):
            for f in range(F):
                ub[f, c, at : at + 2, :] = jnp.zeros((2, N), jnp.bfloat16)
            return carry

        def run():
            lax.fori_loop(0, COLS + 4, body, 0)

        return run

    pl.when(jnp.logical_not(not_first))(clear(0))
    pl.when(jnp.logical_not(not_last))(clear(2 + ROWS))

    for copy in small:
        copy.wait()
    for f in range(F):
        wide = jnp.concatenate([bgv[f].astype(jnp.float32), jnp.zeros((ROWS, 3 * N - COLS), jnp.float32)], axis=1)
        for g in range(COLS // GROUP):
            bt[f, g] = wide[:, g * GROUP : g * GROUP + N]
    gram[...] = jnp.zeros_like(gram)

    def field(f, carry):
        if "convert" in phases:
            def convert(c, carry):
                for k in range(92):
                    fu[c * 92 + k, 0:WIN] = ub[f, c * 92 + k].astype(jnp.float32)[:WIN]
                return carry

            lax.fori_loop(0, (COLS + 4) // 92, convert, 0)

        if "first" in phases:
            def first(g, carry):
                c0 = g * 91
                for t in range(5):
                    at = slice(t * 8 + 1, t * 8 + 9)
                    ca, ck, mask = cf[0, t * 8 : t * 8 + 8], cf[1, t * 8 : t * 8 + 8], cf[2, t * 8 : t * 8 + 8]
                    centre = [fu[c0 + k, at] for k in range(93)]
                    for k in range(91):
                        up, down = fu[c0 + k + 1, t * 8 : t * 8 + 8], fu[c0 + k + 1, t * 8 + 2 : t * 8 + 10]
                        out = ca * centre[k + 1] + ck * (centre[k] + centre[k + 2]) + (up + down)
                        if t in (0, 4):
                            out = out * mask
                        s1[c0 + k, t * 8 : t * 8 + 8] = out
                return carry

            lax.fori_loop(0, (COLS + 2) // 91, first, 0)

        if "second" in phases:
            def second(g, carry):
                c0 = g * GROUP
                lane = lax.broadcasted_iota(jnp.int32, (ROWS, N), 1)
                rows_bg = bt[f, g]
                ones = jnp.ones((N, N), jnp.bfloat16)
                spread = jnp.concatenate([jnp.where(lane == k, rows_bg, 0.0).astype(jnp.bfloat16) for k in range(GROUP)], axis=0)
                grounds = jnp.dot(spread, ones, preferred_element_type=jnp.float32)
                for k in range(GROUP):
                    mid = slice(1, 1 + ROWS)
                    ground = grounds[k * ROWS : (k + 1) * ROWS]
                    out = cf[0, mid] * s1[c0 + k + 1, mid] + cf[1, mid] * (s1[c0 + k, mid] + s1[c0 + k + 2, mid])
                    out = out + (s1[c0 + k + 1, 0:ROWS] + s1[c0 + k + 1, 2 : 2 + ROWS])
                    a_buf[f, c0 + k] = ((out - ground * 25.0) * cf[3, 0:ROWS]).astype(jnp.bfloat16)
                return carry

            lax.fori_loop(0, COLS // GROUP, second, 0)
        if "gram" in phases:
            GC = 180
            def addg(g, carry):
                block = a_buf[f, pl.ds(g * GC, GC)].reshape(GC * ROWS, N)
                gram[...] += lax.dot_general(block, block, (((0,), (0,)), ((), ())), preferred_element_type=jnp.float32)
                return carry
            lax.fori_loop(0, COLS // GC, addg, 0)
        return carry

    stores = []
    for f in range(F):
        if "nodma" not in phases:
            loads[f].wait()
        finish(f)
        field(f, 0)
        store = pltpu.make_async_copy(a_buf.at[f], a_out.at[f], out_sem.at[f])
        if "nodma" not in phases:
            store.start()
            stores.append(store)

    row = lax.broadcasted_iota(jnp.int32, (N, N), 0)
    col = lax.broadcasted_iota(jnp.int32, (N, N), 1)
    work[:, N:] = (row == col).astype(jnp.float32)
    if remote:
        size = N // n_lon
        scatter = []
        for d in range(1, n_lon):
            peer = lax.rem(lon + d, n_lon)
            copy = pltpu.make_async_remote_copy(
                src_ref=gram.at[pl.ds(pl.multiple_of(peer * size, size), size), :],
                dst_ref=got1.at[n_lon - 1 - d],
                send_sem=s1_sem.at[d],
                recv_sem=r1_sem.at[d],
                device_id={"lon": peer, "lat": lat},
                device_id_type=MESH,
            )
            copy.start()
            scatter.append(copy)
        mine = pl.ds(pl.multiple_of(lon * size, size), size)
        acc = gram[mine, :]
        for copy in scatter:
            copy.wait()
        for d in range(n_lon - 1):
            acc = acc + got1[d]
        part[...] = acc
        exchange = []
        for d in range(1, n_lat):
            copy = pltpu.make_async_remote_copy(
                src_ref=part,
                dst_ref=got2.at[lat],
                send_sem=s2_sem.at[d],
                recv_sem=r2_sem.at[d],
                device_id={"lon": lon, "lat": lax.rem(lat + d, n_lat)},
                device_id_type=MESH,
            )
            copy.start()
            exchange.append(copy)
        got2[lat] = acc
        for copy in exchange:
            copy.wait()
        acc = got2[0]
        for d in range(1, n_lat):
            acc = acc + got2[d]
        work[mine, 0:N] = acc / total
        gather = []
        for d in range(1, n_lon):
            copy = pltpu.make_async_remote_copy(
                src_ref=work.at[mine, 0:N],
                dst_ref=work.at[mine, 0:N],
                send_sem=s3_sem.at[d],
                recv_sem=r3_sem.at[d],
                device_id={"lon": lax.rem(lon + d, n_lon), "lat": lat},
                device_id_type=MESH,
            )
            copy.start()
            gather.append(copy)
        for copy in gather:
            copy.wait()
    else:
        work[:, 0:N] = gram[...] / total

    if "chol" in phases:
        eliminate(work)
    r_ref[...] = jnp.where(row <= col, work[:, :N], 0.0)
    inverse = jnp.where(row >= col, work[:, N:], 0.0).T
    hi, mid, lo = split3(inverse)
    w_out[0:N, 0:N] = hi
    w_out[N:, 0:N] = mid
    w_out[0:N, N:] = lo
    w_out[N:, N:] = jnp.zeros((N, N), jnp.bfloat16)
    for store in stores:
        store.wait()


def modes_kernel(a_ref, w_ref, r_in, o_ref, r_out):
    r_out[...] = r_in[...]
    a = a_ref[...]
    out = jnp.dot(jnp.concatenate([a, a], axis=1), w_ref[...], preferred_element_type=jnp.float32)
    o_ref[...] = out[:, :N] + out[:, N:]


ALL = ("convert", "first", "second", "gram", "chol")


def basis(n_lon, n_lat, members, background, remote=True, phases=ALL):
    coefs = jnp.asarray(np.ascontiguousarray(np.broadcast_to(row_table(n_lat * ROWS)[..., None], (n_lat, 4, WIN, N))))
    size = N // n_lon
    vmem, anywhere = pl.BlockSpec(memory_space=pltpu.VMEM), pl.BlockSpec(memory_space=pl.ANY)
    dma = pltpu.SemaphoreType.DMA
    return pl.pallas_call(
        functools.partial(basis_kernel, n_lon, n_lat, float(F * ROWS * COLS * n_lon * n_lat), remote, phases),
        out_shape=[
            jax.ShapeDtypeStruct((F, COLS, ROWS, N), jnp.bfloat16),
            jax.ShapeDtypeStruct((N, N), jnp.float32),
            jax.ShapeDtypeStruct((2 * N, 2 * N), jnp.bfloat16),
        ],
        in_specs=[pl.BlockSpec(memory_space=pltpu.HBM)]*3,
        out_specs=[anywhere, vmem, vmem],
        scratch_shapes=[
            pltpu.VMEM((F, COLS + 4, PACK, N), jnp.bfloat16),
            pltpu.VMEM((COLS + 4, WIN + 8, N), jnp.float32),
            pltpu.VMEM((COLS + 2, WIN, N), jnp.float32),
            pltpu.VMEM((F, COLS, ROWS, N), jnp.bfloat16),
            pltpu.VMEM((F, COLS // GROUP, ROWS, N), jnp.float32),
            pltpu.VMEM((4, WIN, N), jnp.float32),
            pltpu.VMEM((N, N), jnp.float32),
            pltpu.VMEM((size, N), jnp.float32),
            pltpu.VMEM((n_lon, size, N), jnp.float32),
            pltpu.VMEM((n_lat, size, N), jnp.float32),
            pltpu.VMEM((N, 2 * N), jnp.float32),
            pltpu.VMEM((F, ROWS, COLS), jnp.bfloat16),
            dma((F,)),
            dma((2,)),
            dma((F, 8)),
            dma((F, 8)),
            dma((n_lon,)),
            dma((n_lon,)),
            dma((n_lat,)),
            dma((n_lat,)),
            dma((n_lon,)),
            dma((n_lon,)),
            dma((F,)),
        ],
        compiler_params=pltpu.CompilerParams(
            collective_id=0 if remote else None, has_side_effects=True, vmem_limit_bytes=40 * 1024 * 1024
        ),
        name="basis",
    )(pltpu.with_memory_space_constraint(members, pltpu.HBM), pltpu.with_memory_space_constraint(background, pltpu.HBM), pltpu.with_memory_space_constraint(coefs, pltpu.HBM))


def local(n_lon, n_lat, members, background):
    anomaly, r_factor, weights = basis(n_lon, n_lat, jnp.transpose(members, (0, 2, 1, 3)), background)
    total = F * COLS * ROWS
    steps = 12
    modes, r_factor = pl.pallas_call(
        modes_kernel,
        grid=(steps,),
        out_shape=[jax.ShapeDtypeStruct((total, N), jnp.float32), jax.ShapeDtypeStruct((N, N), jnp.float32)],
        in_specs=[
            pl.BlockSpec((total // steps, N), lambda i: (i, 0)),
            pl.BlockSpec((2 * N, 2 * N), lambda i: (0, 0)),
            pl.BlockSpec((N, N), lambda i: (0, 0)),
        ],
        out_specs=[pl.BlockSpec((total // steps, N), lambda i: (i, 0)), pl.BlockSpec((N, N), lambda i: (0, 0))],
        compiler_params=pltpu.CompilerParams(vmem_limit_bytes=16 * 1024 * 1024),
        name="modes",
    )(anomaly.reshape(total, N), weights, r_factor)
    return (jnp.transpose(modes.reshape(F, COLS, ROWS, N), (0, 2, 1, 3)), r_factor)


def solution(mesh):
    return jax.shard_map(
        functools.partial(local, mesh.shape["lon"], mesh.shape["lat"]),
        mesh=mesh,
        in_specs=(P(None, "lat", "lon", None), P(None, "lat", "lon")),
        out_specs=(P(None, "lat", "lon", None), P()),
        check_vma=False,
    )
```

time: 306 us -> 56.2 us (0.18)
  waiting for transfers between devices: 223 us -> 0 us
  Pallas kernels: 6.87 us -> 55.5 us
  other arithmetic: 23.5 us -> 0 us
  starting transfers between devices: 19.3 us -> 0 us
  between operations: 14.2 us -> 0.64 us
  matrix products: 10 us -> 0 us
  local copies, waits for them, and re-layouts: 8.56 us -> 0 us
    psum x2 -> x0, waiting for transfers between devices: 207 us -> none  [the longest x1 133 us: local(): gram = lax.psum(gram, 'lon')]
    pallas_call x1 -> x2, Pallas kernels: 6.87 us -> 55.5 us  [the longest x1 47.8 us: basis(): pl.pallas_call(functools.partial(basis_kernel, n_lon, n_lat, float(F * RO...]
    ppermute x8 -> x0, starting transfers between devices: 19.1 us -> none  [the longest x4 16.3 us: extended(): before = lax.ppermute(last, axis, up)]
    ppermute x8 -> x0, waiting for transfers between devices: 16.2 us -> none  [the longest x4 9.69 us: extended(): after = lax.ppermute(leading, axis, down)]
    convert_element_type x3 -> x0, other arithmetic: 16 us -> none  [the longest x1 14 us: local(): anomaly = ((final - background.astype(jnp.float32)[:, :, :, None]) * weig...]
    dot_general x2 -> x0, matrix products: 10 us -> none  [the longest x1 8 us: local(): jnp.dot(matrix, inverse_t.T, precision=lax.Precision.HIGHEST, preferred_e...]
    unnamed x8 -> x0, local copies, waits for them, and re-layouts: 6.38 us -> none
    add x2 -> x0, other arithmetic: 5.89 us -> none  [the longest x1 5.84 us: smooth_pass(): return centre + kx[None, :, None, None] * east_west + 0.2 * north_south]
  transfers between devices with their start and end apart: 10 -> 0, of which waited for: 8 -> 0; matrix products, arithmetic and copies ran while one was open for 1% -> 0% of each run, Pallas kernels for 0% -> 0%
where the time goes in v3:
time: 56.2 us; the launch traced here: 56.1 us
  Pallas kernels  55.5 us (99%)
  between operations  0.64 us (1%)
    pallas_call x1, Pallas kernels, basis(): pl.pallas_call(functools.partial(basis_kernel, n_lon, n_lat, float(F * RO...  47.8 us
    pallas_call x1, Pallas kernels, local(): pl.pallas_call(modes_kernel, grid=(steps,), out_shape=[jax.ShapeDtypeStru...  7.68 us

profile of v3, /device:TPU:1, one launch (start us, length us, event | category | flops | bytes accessed | tf_op | source)
XLA Modules:
  0.0 56.1 jit_solution(9947986292094099947)
XLA Ops:
  0.6 47.8 %basis.1 = (bf16[3,180,32,128]{3,2,1,0:T(8,128)(2,1)S(1)}, f32[128,128]{1,0:T(8,128)S(1)}, bf16[256,256]{1,0:T(8,128)(2,1)S(1)}) custom-call(bf16[3,180,32,128]{3,2,1,0:T(8,128)(2,1)} %bitcast.6, bf16[3,32,180]{2,1,0:T(8,128)(2,1)} %bg_ref.1, f32[8,4,40,128]{3,2,1,0:T(8,128)} %constant.2.clone.coef_ref), custom_call_target="tpu_custom_call" | custom-call | tf_op jit(solution)/shard_map/basis/pallas_call | solution.py:321
  48.4 7.7 %modes.1 = (f32[17280,128]{1,0:T(8,128)}, f32[128,128]{1,0:T(8,128)}) custom-call(bf16[17280,128]{1,0:T(8,128)(2,1)S(1)} %bitcast.5, bf16[256,256]{1,0:T(8,128)(2,1)S(1)} %get-tuple-element.8.w_ref, f32[128,128]{1,0:T(8,128)S(1)} %get-tuple-element.9.r_in), custom_call_target="tpu_custom_call" | custom-call | tf_op jit(solution)/shard_map/modes/pallas_call | solution.py:366

commit v4 on v1

v4 whole, which is shorter than its diff:
```python
import functools
import math

import jax
import jax.numpy as jnp
import numpy as np
from jax import lax
from jax.experimental import pallas as pl
from jax.experimental.pallas import tpu as pltpu
from jax.sharding import PartitionSpec as P

N = 128
B = 8
F, ROWS, COLS = 3, 32, 180
GROUP = 60
WIN = 40
SIZES = (960,) * 18
MESH = pl.DeviceIdType.MESH


def split3(x):
    hi = x.astype(jnp.bfloat16)
    rest = x - hi.astype(jnp.float32)
    mid = rest.astype(jnp.bfloat16)
    lo = (rest - mid.astype(jnp.float32)).astype(jnp.bfloat16)
    return (hi, mid, lo)


def eliminate(w_ref):
    for b0 in range(0, N, B):
        rows = [w_ref[b0 + j : b0 + j + 1, :] for j in range(B)]
        d = {}
        for i in range(B):
            for j in range(i, B):
                d[i, j] = jnp.broadcast_to(rows[i][:, b0 + j : b0 + j + 1], (1, N))
        for j in range(B):
            s = lax.rsqrt(d[j, j])
            u = rows[j] * jnp.concatenate([s, s], axis=1)
            w_ref[b0 + j : b0 + j + 1, :] = u
            l = {i: d[j, i] * s for i in range(j + 1, B)}
            for i in range(j + 1, B):
                for m in range(i, B):
                    d[i, m] = d[i, m] - l[i] * l[m]
                rows[i] = rows[i] - jnp.concatenate([l[i], l[i]], axis=1) * u
        if b0 + B < N:
            hi, mid, lo = split3(w_ref[b0 : b0 + B, :])
            lhs = jnp.concatenate([hi, hi, mid, hi, lo, mid], axis=0)[:, :N]
            rhs = jnp.concatenate([hi, mid, hi, lo, hi, mid], axis=0)
            update = lax.dot_general(
                lhs, rhs, (((0,), (0,)), ((), ())), preferred_element_type=jnp.float32
            )
            w_ref[b0 + B :, :] = w_ref[b0 + B :, :] - update[b0 + B :, :]


def row_table(nlat):
    glob = np.arange(nlat // ROWS)[:, None] * ROWS + np.arange(-1, WIN - 1)[None, :]

    def of(rows):
        phi = (0.125 * (rows + 0.5) - 0.0625 * nlat) * (math.pi / 180.0)
        return 0.05 + 0.2 * (1.0 - np.cos(phi)), np.sqrt(np.cos(phi))

    kx, _ = of(glob)
    _, weight = of(glob + 1)
    inside = ((glob >= 0) & (glob < nlat)).astype(np.float64)
    table = np.stack([3.0 - 10.0 * kx, 5.0 * kx, inside, 0.04 * weight], axis=1)
    return table.astype(np.float32)


def basis_kernel(
    n_lon, n_lat, total,
    m_ref, bg_ref, coef_ref, a_buf, r_ref, w_out,
    ub, top, bottom, fu, s1, bt, cf, gram, part, got1, got2, work, bgv,
    load_sem, small_sem, hs_sem, hr_sem, s1_sem, r1_sem, s2_sem, r2_sem, s3_sem, r3_sem,
):
    lon, lat = lax.axis_index("lon"), lax.axis_index("lat")
    loads = [
        pltpu.make_async_copy(m_ref.at[f], ub.at[f, pl.ds(2, COLS)], load_sem.at[f])
        for f in range(F)
    ]
    small = [
        pltpu.make_async_copy(bg_ref, bgv, small_sem.at[0]),
        pltpu.make_async_copy(coef_ref.at[lat], cf, small_sem.at[1]),
    ]
    for copy in loads[:1] + small + loads[1:]:
        copy.start()
    not_first, not_last = lat > 0, lat < n_lat - 1
    east, west = lax.rem(lon + 1, n_lon), lax.rem(lon + n_lon - 1, n_lon)
    north, south = lax.rem(lat + n_lat - 1, n_lat), lax.rem(lat + 1, n_lat)

    core, y = lax.rem(lon, 2), lon // 4
    x, z = lax.rem(lat, 4), lax.rem(lon // 2, 2) * 2 + lat // 4

    def in_pair(d):
        core2, x2 = lax.rem(core + d % 2, 2), lax.rem(x + d // 2, 4)
        return core2 + 2 * x2, {"lon": lon - core + core2, "lat": lat - x + x2}

    def in_plane(d):
        y2, z2 = lax.rem(y + d // 4, 4), lax.rem(z + d % 4, 4)
        return {"lon": y2 * 4 + z2 // 2 * 2 + core, "lat": lax.rem(z2, 2) * 4 + x}

    barrier = pltpu.get_barrier_semaphore()
    peers = [{"lon": a, "lat": b} for a in (east, west) for b in (north, south)]
    peers += [{"lon": a, "lat": lat} for a in (east, west)] + [{"lon": lon, "lat": b} for b in (north, south)]
    peers += [in_plane(d) for d in range(1, 16)] + [in_pair(d)[1] for d in range(1, 8)]
    for peer in peers:
        pl.semaphore_signal(barrier, inc=1, device_id=peer, device_id_type=MESH)

    def clear(ref):
        def body(c, carry):
            for f in range(F):
                ref[f, c] = jnp.zeros((2, N), jnp.bfloat16)
            return carry

        def run():
            lax.fori_loop(0, COLS + 4, body, 0)

        return run

    pl.when(jnp.logical_not(not_first))(clear(top))
    pl.when(jnp.logical_not(not_last))(clear(bottom))

    for copy in small:
        copy.wait()
    for f in range(F):
        wide = jnp.concatenate([bgv[f].astype(jnp.float32), jnp.zeros((ROWS, 3 * N - COLS), jnp.float32)], axis=1)
        for g in range(COLS // GROUP):
            bt[f, g] = wide[:, g * GROUP : g * GROUP + N]
    gram[...] = jnp.zeros_like(gram)
    lane = lax.broadcasted_iota(jnp.int32, (16, N), 1)
    ones = jnp.ones((N, N), jnp.bfloat16)

    def first_rows(f, c, t):
        at = pl.ds(8 * t + 7, 8)
        ca, ck = cf[0, 8 * t : 8 * t + 8], cf[1, 8 * t : 8 * t + 8]
        out = ca * fu[f, c + 2, at] + ck * (fu[f, c + 1, at] + fu[f, c + 3, at])
        out = out + (fu[f, c + 2, 8 * t + 6 : 8 * t + 14] + fu[f, c + 2, 8 * t + 8 : 8 * t + 16])
        if t in (0, 4):
            out = out * cf[2, 8 * t : 8 * t + 8]
        s1[f, c + 1, 8 * t : 8 * t + 8] = out

    def second_rows(f, c, t, ground):
        at = slice(8 * t + 1, 8 * t + 9)
        ca, ck, cw = cf[0, at], cf[1, at], cf[3, 8 * t : 8 * t + 8]
        out = ca * s1[f, c + 1, at] + ck * (s1[f, c, at] + s1[f, c + 2, at])
        out = out + (s1[f, c + 1, 8 * t : 8 * t + 8] + s1[f, c + 1, 8 * t + 2 : 8 * t + 10])
        return (out - ground * 25.0) * cw

    def spread(f, g, ks, rows):
        values = jnp.concatenate([bt[f, g, r : r + 8] for r in rows], axis=0)
        picked = [jnp.where(lane == k, values, 0.0).astype(jnp.bfloat16) for k in ks]
        return jnp.dot(jnp.concatenate(picked, axis=0), ones, preferred_element_type=jnp.float32)

    def before(f):
        def widen(i, carry):
            for k in range(90):
                c = i * 90 + k + 2
                fu[f, c, 8 : 8 + ROWS] = ub[f, c].astype(jnp.float32)
            return carry

        lax.fori_loop(0, COLS // 90, widen, 0)

        def first(i, carry):
            for t in (1, 2, 3):
                for k in range(91):
                    first_rows(f, i * 91 + k - 1, t)
            return carry

        lax.fori_loop(0, (COLS + 2) // 91, first, 0)

        def second(g, carry):
            ground = spread(f, g, range(GROUP), (8, 16))
            for k in range(GROUP):
                c = g * GROUP + k
                for t in (1, 2):
                    at = 16 * k + 8 * (t - 1)
                    fu[f, c + 2, 8 * t + 8 : 8 * t + 16] = second_rows(f, c, t, ground[at : at + 8])
            return carry

        lax.fori_loop(0, COLS // GROUP, second, 0)

    def after(f):
        for i in (0, 1, 2, 3, COLS, COLS + 1, COLS + 2, COLS + 3):
            fu[f, i, 8 : 8 + ROWS] = ub[f, i].astype(jnp.float32)
        for c in (-1, 0, COLS - 1, COLS):
            for t in (1, 2, 3):
                first_rows(f, c, t)
        for g, ks in ((0, (0, 1)), (COLS // GROUP - 1, (GROUP - 2, GROUP - 1))):
            ground = spread(f, g, ks, (8, 16))
            for i, k in enumerate(ks):
                c = g * GROUP + k
                for t in (1, 2):
                    at = 16 * i + 8 * (t - 1)
                    fu[f, c + 2, 8 * t + 8 : 8 * t + 16] = second_rows(f, c, t, ground[at : at + 8])

        def widen(i, carry):
            for k in range(91):
                c = i * 91 + k + 1
                fu[f, c, 6:8] = top[f, c].astype(jnp.float32)
                fu[f, c, 8 + ROWS : 10 + ROWS] = bottom[f, c].astype(jnp.float32)
            return carry

        lax.fori_loop(0, (COLS + 2) // 91, widen, 0)

        def first(i, carry):
            for t in (0, 4):
                for k in range(91):
                    first_rows(f, i * 91 + k - 1, t)
            return carry

        lax.fori_loop(0, (COLS + 2) // 91, first, 0)

        def second(g, carry):
            ground = spread(f, g, range(GROUP), (0, 24))
            for k in range(GROUP):
                c = g * GROUP + k
                head = second_rows(f, c, 0, ground[16 * k : 16 * k + 8])
                tail = second_rows(f, c, 3, ground[16 * k + 8 : 16 * k + 16])
                whole = jnp.concatenate([head, fu[f, c + 2, 16:32], tail], axis=0)
                a_buf[f, c] = whole.astype(jnp.bfloat16)
            return carry

        lax.fori_loop(0, COLS // GROUP, second, 0)
        block = a_buf[f].reshape(COLS * ROWS, N)
        gram[...] += lax.dot_general(block, block, (((0,), (0,)), ((), ())), preferred_element_type=jnp.float32)

    loads[0].wait()
    before(0)
    pl.semaphore_wait(barrier, len(peers))

    everyone = (None, None)
    down, up = (not_last, not_first), (not_first, not_last)
    fields, cols = pl.ds(0, F), pl.ds(2, COLS)
    left, right, left1, right1 = pl.ds(0, 2), pl.ds(2 + COLS, 2), pl.ds(1, 1), pl.ds(2 + COLS, 1)
    last2, last1, head2, head1 = pl.ds(COLS - 2, 2), pl.ds(COLS - 1, 1), pl.ds(0, 2), pl.ds(0, 1)
    all_rows, first_two, last_two = pl.ds(0, ROWS), pl.ds(0, 2), pl.ds(ROWS - 2, 2)

    def rows_of(f):
        return [
            (pl.ds(f, 1), pl.ds(0, COLS), last_two, top, cols, lon, south, down),
            (pl.ds(f, 1), pl.ds(0, COLS), first_two, bottom, cols, lon, north, up),
        ]

    plan = rows_of(0) + [
        (fields, last2, all_rows, ub, left, east, lat, everyone),
        (fields, head2, all_rows, ub, right, west, lat, everyone),
        (fields, last1, last_two, top, left1, east, south, down),
        (fields, head1, last_two, top, right1, west, south, down),
        (fields, last1, first_two, bottom, left1, east, north, up),
        (fields, head1, first_two, bottom, right1, west, north, up),
    ] + rows_of(1) + rows_of(2)
    halos = []
    for i, (fs, sc, sr, ref, dc, a, b, (send, receive)) in enumerate(plan):
        copy = pltpu.make_async_remote_copy(
            src_ref=m_ref.at[fs, sc, sr, :],
            dst_ref=ref.at[fs, dc],
            send_sem=hs_sem.at[i],
            recv_sem=hr_sem.at[i],
            device_id={"lon": a, "lat": b},
            device_id_type=MESH,
        )
        halos.append((copy, send, receive))
        if send is None:
            copy.start()
        else:
            pl.when(send)(copy.start)

    def finish(some):
        for copy, send, receive in some:
            if send is None:
                copy.wait()
            else:
                pl.when(receive)(copy.wait_recv)
                pl.when(send)(copy.wait_send)

    for f in (1, 2):
        loads[f].wait()
        before(f)
    for f, some in ((0, halos[:8]), (1, halos[8:10]), (2, halos[10:])):
        finish(some)
        after(f)

    row = lax.broadcasted_iota(jnp.int32, (N, N), 0)
    col = lax.broadcasted_iota(jnp.int32, (N, N), 1)

    size = N // 8

    def rows_at(p):
        return pl.ds(pl.multiple_of(p * size, size), size)

    scatter = []
    for d in range(1, 8):
        place, peer = in_pair(d)
        copy = pltpu.make_async_remote_copy(
            src_ref=gram.at[rows_at(place), :],
            dst_ref=got1.at[d],
            send_sem=s1_sem.at[d],
            recv_sem=r1_sem.at[d],
            device_id=peer,
            device_id_type=MESH,
        )
        copy.start()
        scatter.append(copy)
    mine = rows_at(core + 2 * x)
    work[:, N:] = (row == col).astype(jnp.float32)
    acc = gram[mine, :]
    for copy in scatter:
        copy.wait()
    for d in range(1, 8):
        acc = acc + got1[d]
    part[...] = acc
    slot = y * 4 + z
    exchange = []
    for d in range(1, 16):
        copy = pltpu.make_async_remote_copy(
            src_ref=part,
            dst_ref=got2.at[slot],
            send_sem=s2_sem.at[d],
            recv_sem=r2_sem.at[d],
            device_id=in_plane(d),
            device_id_type=MESH,
        )
        copy.start()
        exchange.append(copy)
    got2[slot] = acc
    for copy in exchange:
        copy.wait()
    sums = [got2[d] for d in range(16)]
    while len(sums) > 1:
        sums = [a + b for a, b in zip(sums[::2], sums[1::2])]
    work[mine, 0:N] = sums[0] / total
    gather = []
    for d in range(1, 8):
        copy = pltpu.make_async_remote_copy(
            src_ref=work.at[mine, 0:N],
            dst_ref=work.at[mine, 0:N],
            send_sem=s3_sem.at[d],
            recv_sem=r3_sem.at[d],
            device_id=in_pair(d)[1],
            device_id_type=MESH,
        )
        copy.start()
        gather.append(copy)
    for copy in gather:
        copy.wait()

    eliminate(work)
    r_ref[...] = jnp.where(row <= col, work[:, :N], 0.0)
    inverse = jnp.where(row >= col, work[:, N:], 0.0).T
    hi, mid, lo = split3(inverse)
    w_out[0:N, 0:N] = hi
    w_out[N:, 0:N] = mid
    w_out[0:N, N:] = lo
    w_out[N:, N:] = jnp.zeros((N, N), jnp.bfloat16)


def modes_kernel(sizes, a_ref, w_ref, r_ref, o_ref, r_out, buf, sem):
    stores, at = [], 0
    for i, size in enumerate(sizes):
        a = a_ref[at : at + size]
        out = jnp.dot(jnp.concatenate([a, a], axis=1), w_ref[...], preferred_element_type=jnp.float32)
        buf[at : at + size] = out[:, :N] + out[:, N:]
        store = pltpu.make_async_copy(buf.at[pl.ds(at, size)], o_ref.at[pl.ds(at, size)], sem.at[i])
        store.start()
        stores.append(store)
        at += size
    r_out[...] = r_ref[...]
    for store in stores:
        store.wait()


def local(n_lon, n_lat, members, background):
    assert n_lon == 16 and n_lat == 8
    coefs = jnp.asarray(np.ascontiguousarray(np.broadcast_to(row_table(n_lat * ROWS)[..., None], (n_lat, 4, WIN, N))))
    vmem, hbm = pl.BlockSpec(memory_space=pltpu.VMEM), pl.BlockSpec(memory_space=pltpu.HBM)
    dma, scratch = pltpu.SemaphoreType.DMA, pltpu.VMEM
    anomaly, r_factor, weights = pl.pallas_call(
        functools.partial(basis_kernel, n_lon, n_lat, float(F * ROWS * COLS * n_lon * n_lat)),
        out_shape=[
            jax.ShapeDtypeStruct((F, COLS, ROWS, N), jnp.bfloat16),
            jax.ShapeDtypeStruct((N, N), jnp.float32),
            jax.ShapeDtypeStruct((2 * N, 2 * N), jnp.bfloat16),
        ],
        in_specs=[hbm, hbm, hbm],
        out_specs=[vmem, vmem, vmem],
        scratch_shapes=[
            scratch((F, COLS + 4, ROWS, N), jnp.bfloat16),
            scratch((F, COLS + 4, 2, N), jnp.bfloat16),
            scratch((F, COLS + 4, 2, N), jnp.bfloat16),
            scratch((F, COLS + 4, WIN + 8, N), jnp.float32),
            scratch((F, COLS + 2, WIN, N), jnp.float32),
            scratch((F, COLS // GROUP, ROWS, N), jnp.float32),
            scratch((4, WIN, N), jnp.float32),
            scratch((N, N), jnp.float32),
            scratch((N // 8, N), jnp.float32),
            scratch((8, N // 8, N), jnp.float32),
            scratch((16, N // 8, N), jnp.float32),
            scratch((N, 2 * N), jnp.float32),
            scratch((F, ROWS, COLS), jnp.bfloat16),
            dma((F,)), dma((2,)), dma((12,)), dma((12,)),
            dma((8,)), dma((8,)), dma((16,)), dma((16,)), dma((8,)), dma((8,)),
        ],
        compiler_params=pltpu.CompilerParams(
            collective_id=0, has_side_effects=True, vmem_limit_bytes=42 * 1024 * 1024
        ),
        name="basis",
    )(*(pltpu.with_memory_space_constraint(a, pltpu.HBM) for a in (jnp.transpose(members, (0, 2, 1, 3)), background, coefs)))
    total = F * COLS * ROWS
    sizes = SIZES
    modes, r_factor = pl.pallas_call(
        functools.partial(modes_kernel, sizes),
        out_shape=[jax.ShapeDtypeStruct((total, N), jnp.float32), jax.ShapeDtypeStruct((N, N), jnp.float32)],
        in_specs=[vmem, vmem, vmem],
        out_specs=[hbm, vmem],
        scratch_shapes=[scratch((total, N), jnp.float32), dma((len(sizes),))],
        compiler_params=pltpu.CompilerParams(vmem_limit_bytes=24 * 1024 * 1024),
        name="modes",
    )(anomaly.reshape(total, N), weights, r_factor)
    return (jnp.transpose(modes.reshape(F, COLS, ROWS, N), (0, 2, 1, 3)), r_factor)


def solution(mesh):
    return jax.shard_map(
        functools.partial(local, mesh.shape["lon"], mesh.shape["lat"]),
        mesh=mesh,
        in_specs=(P(None, "lat", "lon", None), P(None, "lat", "lon")),
        out_specs=(P(None, "lat", "lon", None), P()),
        check_vma=False,
    )
```

time: 306 us -> 49.4 us (0.16)
  waiting for transfers between devices: 223 us -> 0 us
  Pallas kernels: 6.87 us -> 48.6 us
  other arithmetic: 23.5 us -> 0 us
  starting transfers between devices: 19.3 us -> 0 us
  between operations: 14.2 us -> 0.64 us
  matrix products: 10 us -> 0 us
  local copies, waits for them, and re-layouts: 8.56 us -> 0 us
    psum x2 -> x0, waiting for transfers between devices: 207 us -> none  [the longest x1 133 us: local(): gram = lax.psum(gram, 'lon')]
    pallas_call x1 -> x2, Pallas kernels: 6.87 us -> 48.6 us  [the longest x1 44 us: local(): pl.pallas_call(functools.partial(basis_kernel, n_lon, n_lat, float(F * RO...]
    ppermute x8 -> x0, starting transfers between devices: 19.1 us -> none  [the longest x4 16.3 us: extended(): before = lax.ppermute(last, axis, up)]
    ppermute x8 -> x0, waiting for transfers between devices: 16.2 us -> none  [the longest x4 9.69 us: extended(): after = lax.ppermute(leading, axis, down)]
    convert_element_type x3 -> x0, other arithmetic: 16 us -> none  [the longest x1 14 us: local(): anomaly = ((final - background.astype(jnp.float32)[:, :, :, None]) * weig...]
    dot_general x2 -> x0, matrix products: 10 us -> none  [the longest x1 8 us: local(): jnp.dot(matrix, inverse_t.T, precision=lax.Precision.HIGHEST, preferred_e...]
    unnamed x8 -> x0, local copies, waits for them, and re-layouts: 6.38 us -> none
    add x2 -> x0, other arithmetic: 5.89 us -> none  [the longest x1 5.84 us: smooth_pass(): return centre + kx[None, :, None, None] * east_west + 0.2 * north_south]
  transfers between devices with their start and end apart: 10 -> 0, of which waited for: 8 -> 0; matrix products, arithmetic and copies ran while one was open for 1% -> 0% of each run, Pallas kernels for 0% -> 0%
where the time goes in v4:
time: 49.4 us; the launch traced here: 49.3 us
  Pallas kernels  48.6 us (98%)
  between operations  0.64 us (1%)
    pallas_call x1, Pallas kernels, local(): pl.pallas_call(functools.partial(basis_kernel, n_lon, n_lat, float(F * RO...  44 us
    pallas_call x1, Pallas kernels, local(): pl.pallas_call(functools.partial(modes_kernel, sizes), out_shape=[jax.Sha...  4.62 us

profile of v4, /device:TPU:1, one launch (start us, length us, event | category | flops | bytes accessed | tf_op | source)
XLA Modules:
  0.0 49.3 jit_solution(11009199276463476305)
XLA Ops:
  0.6 44.0 %basis.1 = (bf16[3,180,32,128]{3,2,1,0:T(8,128)(2,1)S(1)}, f32[128,128]{1,0:T(8,128)S(1)}, bf16[256,256]{1,0:T(8,128)(2,1)S(1)}) custom-call(bf16[3,180,32,128]{3,2,1,0:T(8,128)(2,1)} %bitcast.6, bf16[3,32,180]{2,1,0:T(8,128)(2,1)} %bg_ref.1, f32[8,4,40,128]{3,2,1,0:T(8,128)} %constant.2.clone.coef_ref), custom_call_target="tpu_custom_call" | custom-call | tf_op jit(solution)/shard_map/basis/pallas_call | solution.py:376
  44.7 4.6 %modes.1 = (f32[17280,128]{1,0:T(8,128)}, f32[128,128]{1,0:T(8,128)}) custom-call(bf16[17280,128]{1,0:T(8,128)(2,1)S(1)} %bitcast.5, bf16[256,256]{1,0:T(8,128)(2,1)S(1)} %get-tuple-element.8.w_ref, f32[128,128]{1,0:T(8,128)S(1)} %get-tuple-element.9.r_ref), custom_call_target="tpu_custom_call" | custom-call | tf_op jit(solution)/shard_map/modes/pallas_call | solution.py:409

commit v5 on v4

--- a/solution.py
+++ b/solution.py
@@ -10,10 +10,11 @@
 from jax.sharding import PartitionSpec as P
 
 N = 128
-B = 8
+B = 16
 F, ROWS, COLS = 3, 32, 180
 GROUP = 60
 WIN = 40
+GROUPS = COLS // GROUP
 SIZES = (960,) * 18
 MESH = pl.DeviceIdType.MESH
 
@@ -69,7 +70,7 @@
 def basis_kernel(
     n_lon, n_lat, total,
     m_ref, bg_ref, coef_ref, a_buf, r_ref, w_out,
-    ub, top, bottom, fu, s1, bt, cf, gram, part, got1, got2, work, bgv,
+    ub, edge, fu, s1, bt, hot, cf, gram, part, got1, got2, work, bgv,
     load_sem, small_sem, hs_sem, hr_sem, s1_sem, r1_sem, s2_sem, r2_sem, s3_sem, r3_sem,
 ):
     lon, lat = lax.axis_index("lon"), lax.axis_index("lat")
@@ -105,10 +106,10 @@
     for peer in peers:
         pl.semaphore_signal(barrier, inc=1, device_id=peer, device_id_type=MESH)
 
-    def clear(ref):
+    def clear(at):
         def body(c, carry):
             for f in range(F):
-                ref[f, c] = jnp.zeros((2, N), jnp.bfloat16)
+                edge[f, c, at : at + 2] = jnp.zeros((2, N), jnp.bfloat16)
             return carry
 
         def run():
@@ -116,39 +117,55 @@
 
         return run
 
-    pl.when(jnp.logical_not(not_first))(clear(top))
-    pl.when(jnp.logical_not(not_last))(clear(bottom))
+    pl.when(jnp.logical_not(not_first))(clear(0))
+    pl.when(jnp.logical_not(not_last))(clear(2))
 
     for copy in small:
         copy.wait()
     for f in range(F):
         wide = jnp.concatenate([bgv[f].astype(jnp.float32), jnp.zeros((ROWS, 3 * N - COLS), jnp.float32)], axis=1)
         for g in range(COLS // GROUP):
-            bt[f, g] = wide[:, g * GROUP : g * GROUP + N]
+            part_of = wide[:, g * GROUP : g * GROUP + N]
+            bt[f, g, 0] = part_of[8:24].astype(jnp.bfloat16)
+            bt[f, g, 1] = jnp.concatenate([part_of[0:8], part_of[24:32]], axis=0).astype(jnp.bfloat16)
     gram[...] = jnp.zeros_like(gram)
     lane = lax.broadcasted_iota(jnp.int32, (16, N), 1)
-    ones = jnp.ones((N, N), jnp.bfloat16)
-
-    def first_rows(f, c, t):
-        at = pl.ds(8 * t + 7, 8)
+    for k in range(GROUP):
+        hot[k] = jnp.where(lane == k, 1.0, 0.0).astype(jnp.bfloat16)
+    scale = jnp.full((N, N), -25.0, jnp.bfloat16)
+
+    def first_rows(f, c0, n, t):
+        at = slice(8 * t + 7, 8 * t + 15)
         ca, ck = cf[0, 8 * t : 8 * t + 8], cf[1, 8 * t : 8 * t + 8]
-        out = ca * fu[f, c + 2, at] + ck * (fu[f, c + 1, at] + fu[f, c + 3, at])
-        out = out + (fu[f, c + 2, 8 * t + 6 : 8 * t + 14] + fu[f, c + 2, 8 * t + 8 : 8 * t + 16])
-        if t in (0, 4):
-            out = out * cf[2, 8 * t : 8 * t + 8]
-        s1[f, c + 1, 8 * t : 8 * t + 8] = out
-
-    def second_rows(f, c, t, ground):
+        behind, here = fu[f, c0 + 1, at], fu[f, c0 + 2, at]
+        for k in range(n):
+            c = c0 + k
+            ahead = fu[f, c + 3, at]
+            out = ca * here + ck * (behind + ahead)
+            out = out + (fu[f, c + 2, 8 * t + 6 : 8 * t + 14] + fu[f, c + 2, 8 * t + 8 : 8 * t + 16])
+            if t in (0, 4):
+                out = out * cf[2, 8 * t : 8 * t + 8]
+            s1[f, c + 1, 8 * t : 8 * t + 8] = out
+            behind, here = here, ahead
+
+    def second_rows(f, c0, t):
         at = slice(8 * t + 1, 8 * t + 9)
         ca, ck, cw = cf[0, at], cf[1, at], cf[3, 8 * t : 8 * t + 8]
-        out = ca * s1[f, c + 1, at] + ck * (s1[f, c, at] + s1[f, c + 2, at])
-        out = out + (s1[f, c + 1, 8 * t : 8 * t + 8] + s1[f, c + 1, 8 * t + 2 : 8 * t + 10])
-        return (out - ground * 25.0) * cw
-
-    def spread(f, g, ks, rows):
-        values = jnp.concatenate([bt[f, g, r : r + 8] for r in rows], axis=0)
-        picked = [jnp.where(lane == k, values, 0.0).astype(jnp.bfloat16) for k in ks]
-        return jnp.dot(jnp.concatenate(picked, axis=0), ones, preferred_element_type=jnp.float32)
+        held = [s1[f, c0, at], s1[f, c0 + 1, at]]
+
+        def step(k, ground):
+            c = c0 + k
+            (behind, here), ahead = held, s1[f, c + 2, at]
+            out = ca * here + ck * (behind + ahead)
+            out = out + (s1[f, c + 1, 8 * t : 8 * t + 8] + s1[f, c + 1, 8 * t + 2 : 8 * t + 10])
+            held[:] = [here, ahead]
+            return (out + ground) * cw
+
+        return step
+
+    def spread(f, g, ks, half):
+        picked = [bt[f, g, half] * hot[k] for k in ks]
+        return jnp.dot(jnp.concatenate(picked, axis=0), scale, preferred_element_type=jnp.float32)
 
     def before(f):
         def widen(i, carry):
@@ -161,19 +178,18 @@
 
         def first(i, carry):
             for t in (1, 2, 3):
-                for k in range(91):
-                    first_rows(f, i * 91 + k - 1, t)
+                first_rows(f, i * 91 - 1, 91, t)
             return carry
 
         lax.fori_loop(0, (COLS + 2) // 91, first, 0)
 
         def second(g, carry):
-            ground = spread(f, g, range(GROUP), (8, 16))
-            for k in range(GROUP):
-                c = g * GROUP + k
-                for t in (1, 2):
+            ground = spread(f, g, range(GROUP), 0)
+            for t in (1, 2):
+                step = second_rows(f, g * GROUP, t)
+                for k in range(GROUP):
                     at = 16 * k + 8 * (t - 1)
-                    fu[f, c + 2, 8 * t + 8 : 8 * t + 16] = second_rows(f, c, t, ground[at : at + 8])
+                    fu[f, g * GROUP + k + 2, 8 * t + 8 : 8 * t + 16] = step(k, ground[at : at + 8])
             return carry
 
         lax.fori_loop(0, COLS // GROUP, second, 0)
@@ -181,47 +197,47 @@
     def after(f):
         for i in (0, 1, 2, 3, COLS, COLS + 1, COLS + 2, COLS + 3):
             fu[f, i, 8 : 8 + ROWS] = ub[f, i].astype(jnp.float32)
-        for c in (-1, 0, COLS - 1, COLS):
+        for c in (-1, COLS - 1):
             for t in (1, 2, 3):
-                first_rows(f, c, t)
+                first_rows(f, c, 2, t)
         for g, ks in ((0, (0, 1)), (COLS // GROUP - 1, (GROUP - 2, GROUP - 1))):
-            ground = spread(f, g, ks, (8, 16))
-            for i, k in enumerate(ks):
-                c = g * GROUP + k
-                for t in (1, 2):
+            ground = spread(f, g, ks, 0)
+            c = g * GROUP + ks[0]
+            for t in (1, 2):
+                step = second_rows(f, c, t)
+                for i in range(len(ks)):
                     at = 16 * i + 8 * (t - 1)
-                    fu[f, c + 2, 8 * t + 8 : 8 * t + 16] = second_rows(f, c, t, ground[at : at + 8])
+                    fu[f, c + i + 2, 8 * t + 8 : 8 * t + 16] = step(i, ground[at : at + 8])
 
         def widen(i, carry):
             for k in range(91):
                 c = i * 91 + k + 1
-                fu[f, c, 6:8] = top[f, c].astype(jnp.float32)
-                fu[f, c, 8 + ROWS : 10 + ROWS] = bottom[f, c].astype(jnp.float32)
+                both = edge[f, c].astype(jnp.float32)
+                fu[f, c, 6:8] = both[0:2]
+                fu[f, c, 8 + ROWS : 10 + ROWS] = both[2:4]
             return carry
 
         lax.fori_loop(0, (COLS + 2) // 91, widen, 0)
 
         def first(i, carry):
             for t in (0, 4):
-                for k in range(91):
-                    first_rows(f, i * 91 + k - 1, t)
+                first_rows(f, i * 91 - 1, 91, t)
             return carry
 
         lax.fori_loop(0, (COLS + 2) // 91, first, 0)
 
         def second(g, carry):
-            ground = spread(f, g, range(GROUP), (0, 24))
+            ground = spread(f, g, range(GROUP), 1)
+            heads, tails = second_rows(f, g * GROUP, 0), second_rows(f, g * GROUP, 3)
             for k in range(GROUP):
                 c = g * GROUP + k
-                head = second_rows(f, c, 0, ground[16 * k : 16 * k + 8])
-                tail = second_rows(f, c, 3, ground[16 * k + 8 : 16 * k + 16])
+                head = heads(k, ground[16 * k : 16 * k + 8])
+                tail = tails(k, ground[16 * k + 8 : 16 * k + 16])
                 whole = jnp.concatenate([head, fu[f, c + 2, 16:32], tail], axis=0)
                 a_buf[f, c] = whole.astype(jnp.bfloat16)
             return carry
 
         lax.fori_loop(0, COLS // GROUP, second, 0)
-        block = a_buf[f].reshape(COLS * ROWS, N)
-        gram[...] += lax.dot_general(block, block, (((0,), (0,)), ((), ())), preferred_element_type=jnp.float32)
 
     loads[0].wait()
     before(0)
@@ -236,23 +252,23 @@
 
     def rows_of(f):
         return [
-            (pl.ds(f, 1), pl.ds(0, COLS), last_two, top, cols, lon, south, down),
-            (pl.ds(f, 1), pl.ds(0, COLS), first_two, bottom, cols, lon, north, up),
+            (pl.ds(f, 1), pl.ds(0, COLS), last_two, 0, cols, lon, south, down),
+            (pl.ds(f, 1), pl.ds(0, COLS), first_two, 2, cols, lon, north, up),
         ]
 
     plan = rows_of(0) + [
-        (fields, last2, all_rows, ub, left, east, lat, everyone),
-        (fields, head2, all_rows, ub, right, west, lat, everyone),
-        (fields, last1, last_two, top, left1, east, south, down),
-        (fields, head1, last_two, top, right1, west, south, down),
-        (fields, last1, first_two, bottom, left1, east, north, up),
-        (fields, head1, first_two, bottom, right1, west, north, up),
+        (fields, last2, all_rows, None, left, east, lat, everyone),
+        (fields, head2, all_rows, None, right, west, lat, everyone),
+        (fields, last1, last_two, 0, left1, east, south, down),
+        (fields, head1, last_two, 0, right1, west, south, down),
+        (fields, last1, first_two, 2, left1, east, north, up),
+        (fields, head1, first_two, 2, right1, west, north, up),
     ] + rows_of(1) + rows_of(2)
     halos = []
-    for i, (fs, sc, sr, ref, dc, a, b, (send, receive)) in enumerate(plan):
+    for i, (fs, sc, sr, at, dc, a, b, (send, receive)) in enumerate(plan):
         copy = pltpu.make_async_remote_copy(
             src_ref=m_ref.at[fs, sc, sr, :],
-            dst_ref=ref.at[fs, dc],
+            dst_ref=ub.at[fs, dc] if at is None else edge.at[fs, dc, pl.ds(at, 2), :],
             send_sem=hs_sem.at[i],
             recv_sem=hr_sem.at[i],
             device_id={"lon": a, "lat": b},
@@ -278,6 +294,8 @@
     for f, some in ((0, halos[:8]), (1, halos[8:10]), (2, halos[10:])):
         finish(some)
         after(f)
+        block = a_buf[f].reshape(COLS * ROWS, N)
+        gram[...] += lax.dot_general(block, block, (((0,), (0,)), ((), ())), preferred_element_type=jnp.float32)
 
     row = lax.broadcasted_iota(jnp.int32, (N, N), 0)
     col = lax.broadcasted_iota(jnp.int32, (N, N), 1)
@@ -384,11 +402,11 @@
         out_specs=[vmem, vmem, vmem],
         scratch_shapes=[
             scratch((F, COLS + 4, ROWS, N), jnp.bfloat16),
-            scratch((F, COLS + 4, 2, N), jnp.bfloat16),
-            scratch((F, COLS + 4, 2, N), jnp.bfloat16),
+            scratch((F, COLS + 4, 4, N), jnp.bfloat16),
             scratch((F, COLS + 4, WIN + 8, N), jnp.float32),
             scratch((F, COLS + 2, WIN, N), jnp.float32),
-            scratch((F, COLS // GROUP, ROWS, N), jnp.float32),
+            scratch((F, GROUPS, 2, 16, N), jnp.bfloat16),
+            scratch((GROUP, 16, N), jnp.bfloat16),
             scratch((4, WIN, N), jnp.float32),
             scratch((N, N), jnp.float32),
             scratch((N // 8, N), jnp.float32),

time: 49.4 us -> 48.3 us (0.978)
  Pallas kernels: 48.6 us -> 47.6 us
    pallas_call x1, Pallas kernels: 44 us -> 42.9 us  [local(): pl.pallas_call(functools.partial(basis_kernel, n_lon, n_lat, float(F * RO...]
where the time goes in v5:
time: 48.3 us; the launch traced here: 48.2 us
  Pallas kernels  47.6 us (99%)
  between operations  0.64 us (1%)
    pallas_call x1, Pallas kernels, local(): pl.pallas_call(functools.partial(basis_kernel, n_lon, n_lat, float(F * RO...  42.9 us
    pallas_call x1, Pallas kernels, local(): pl.pallas_call(functools.partial(modes_kernel, sizes), out_shape=[jax.Sha...  4.62 us

profile of v5, /device:TPU:1, one launch (start us, length us, event | category | flops | bytes accessed | tf_op | source)
XLA Modules:
  0.0 48.2 jit_solution(13320664524380833613)
XLA Ops:
  0.6 42.9 %basis.1 = (bf16[3,180,32,128]{3,2,1,0:T(8,128)(2,1)S(1)}, f32[128,128]{1,0:T(8,128)S(1)}, bf16[256,256]{1,0:T(8,128)(2,1)S(1)}) custom-call(bf16[3,180,32,128]{3,2,1,0:T(8,128)(2,1)} %bitcast.6, bf16[3,32,180]{2,1,0:T(8,128)(2,1)} %bg_ref.1, f32[8,4,40,128]{3,2,1,0:T(8,128)} %constant.2.clone.coef_ref), custom_call_target="tpu_custom_call" | custom-call | tf_op jit(solution)/shard_map/basis/pallas_call | solution.py:394
  43.6 4.6 %modes.1 = (f32[17280,128]{1,0:T(8,128)}, f32[128,128]{1,0:T(8,128)}) custom-call(bf16[17280,128]{1,0:T(8,128)(2,1)S(1)} %bitcast.5, bf16[256,256]{1,0:T(8,128)(2,1)S(1)} %get-tuple-element.8.w_ref, f32[128,128]{1,0:T(8,128)S(1)} %get-tuple-element.9.r_ref), custom_call_target="tpu_custom_call" | custom-call | tf_op jit(solution)/shard_map/modes/pallas_call | solution.py:427

commit v6 on v5

--- a/solution.py
+++ b/solution.py
@@ -12,7 +12,7 @@
 N = 128
 B = 16
 F, ROWS, COLS = 3, 32, 180
-GROUP = 60
+GROUP = 90
 WIN = 40
 GROUPS = COLS // GROUP
 SIZES = (960,) * 18
@@ -120,6 +120,12 @@
     pl.when(jnp.logical_not(not_first))(clear(0))
     pl.when(jnp.logical_not(not_last))(clear(2))
 
+    gram[...] = jnp.zeros_like(gram)
+    lane = lax.broadcasted_iota(jnp.int32, (16, N), 1)
+    for k in range(GROUP):
+        hot[k] = jnp.where(lane == k, 1.0, 0.0).astype(jnp.bfloat16)
+    scale = jnp.full((N, N), -25.0, jnp.bfloat16)
+
     for copy in small:
         copy.wait()
     for f in range(F):
@@ -128,12 +134,6 @@
             part_of = wide[:, g * GROUP : g * GROUP + N]
             bt[f, g, 0] = part_of[8:24].astype(jnp.bfloat16)
             bt[f, g, 1] = jnp.concatenate([part_of[0:8], part_of[24:32]], axis=0).astype(jnp.bfloat16)
-    gram[...] = jnp.zeros_like(gram)
-    lane = lax.broadcasted_iota(jnp.int32, (16, N), 1)
-    for k in range(GROUP):
-        hot[k] = jnp.where(lane == k, 1.0, 0.0).astype(jnp.bfloat16)
-    scale = jnp.full((N, N), -25.0, jnp.bfloat16)
-
     def first_rows(f, c0, n, t):
         at = slice(8 * t + 7, 8 * t + 15)
         ca, ck = cf[0, 8 * t : 8 * t + 8], cf[1, 8 * t : 8 * t + 8]

time: 48.3 us -> 48.2 us (level)
  no operation moved by 1% of the time
where the time goes in v6:
time: 48.2 us; the launch traced here: 48.1 us
  Pallas kernels  47.4 us (98%)
  between operations  0.64 us (1%)
    pallas_call x1, Pallas kernels, local(): pl.pallas_call(functools.partial(basis_kernel, n_lon, n_lat, float(F * RO...  42.8 us
    pallas_call x1, Pallas kernels, local(): pl.pallas_call(functools.partial(modes_kernel, sizes), out_shape=[jax.Sha...  4.62 us

profile of v6, /device:TPU:1, one launch (start us, length us, event | category | flops | bytes accessed | tf_op | source)
XLA Modules:
  0.0 48.1 jit_solution(2856621987343159519)
XLA Ops:
  0.6 42.8 %basis.1 = (bf16[3,180,32,128]{3,2,1,0:T(8,128)(2,1)S(1)}, f32[128,128]{1,0:T(8,128)S(1)}, bf16[256,256]{1,0:T(8,128)(2,1)S(1)}) custom-call(bf16[3,180,32,128]{3,2,1,0:T(8,128)(2,1)} %bitcast.6, bf16[3,32,180]{2,1,0:T(8,128)(2,1)} %bg_ref.1, f32[8,4,40,128]{3,2,1,0:T(8,128)} %constant.2.clone.coef_ref), custom_call_target="tpu_custom_call" | custom-call | tf_op jit(solution)/shard_map/basis/pallas_call | solution.py:394
  43.4 4.6 %modes.1 = (f32[17280,128]{1,0:T(8,128)}, f32[128,128]{1,0:T(8,128)}) custom-call(bf16[17280,128]{1,0:T(8,128)(2,1)S(1)} %bitcast.5, bf16[256,256]{1,0:T(8,128)(2,1)S(1)} %get-tuple-element.8.w_ref, f32[128,128]{1,0:T(8,128)S(1)} %get-tuple-element.9.r_ref), custom_call_target="tpu_custom_call" | custom-call | tf_op jit(solution)/shard_map/modes/pallas_call | solution.py:427
